TPU v7x, 32 devices: a whole 2x2x4 slice. The times are simulated.
32 devices in a mesh: seq: 16 (over z, x, core), dp: 2 (over y).
Axes of the slice: x: 2, y: 2, z: 4, core: 2. Of those that a mesh axis runs over, the one named last changes fastest.
Arguments:
- inputs: bfloat16 [2, 2048, 2048], P('dp', 'seq'), may hold values from -6 to 6
- step_sizes: float32 [2, 2048, 32], P('dp', 'seq'), may hold values from 0.5 to 2
- write_vecs: bfloat16 [2, 2048, 64], P('dp', 'seq'), may hold values from -0.29882812 to 0.29882812
- read_vecs: bfloat16 [2, 2048, 64], P('dp', 'seq'), may hold values from -0.29882812 to 0.29882812
- log_rates: float32 [32], replicated, may hold values from -10 to -3.2
- skip_gain: float32 [32], replicated, may hold values from 0.5 to 1.5
- resets: int32 [2, 8], P('dp'), may hold values from 1 to 2047
- cotangent: bfloat16 [2, 2048, 2048], P('dp', 'seq'), may hold values from -3 to 3
Outputs:
- outputs: bfloat16 [2, 2048, 2048], P('dp', 'seq')
- grad_inputs: bfloat16 [2, 2048, 2048], P('dp', 'seq')
- grad_steps: float32 [2, 2048, 32], P('dp', 'seq')
- grad_write: float32 [2, 2048, 64], P('dp', 'seq')
- grad_read: float32 [2, 2048, 64], P('dp', 'seq')
- grad_rates: float32 [32], replicated
- grad_skip: float32 [32], replicated
All inputs are finite; a program needn't handle non-finite values.
Results may differ from a plain program's by a relative error of at most 0.0044.
Values sent between devices are 32-bit elements; how exact they have to be, the bound alone decides.
No kernel may reach another device: no remote copies, remote signals or barrier semaphores. Data moves between devices by JAX's collectives and lax.ppermute only.
A program may use at most 256 MiB of HBM per device.

v0:
```python
import jax
import jax.numpy as jnp
from jax import lax
from jax.sharding import PartitionSpec as P

PRECISE = lax.Precision.HIGH


def prefix(value, axis, join, neutral, backward):
    count, mine = (lax.axis_size(axis), lax.axis_index(axis))
    pieces = jax.tree.map(lambda part: lax.all_gather(part, axis), value)
    if backward:
        pieces = jax.tree.map(lambda part: part[::-1], pieces)
        mine = count - 1 - mine
    subtotal = jax.tree.map(
        lambda part, zero: jnp.full_like(part, 0) + jnp.asarray(zero, part.dtype), value, neutral
    )

    def hop(position, subtotal):
        longer = join(subtotal, jax.tree.map(lambda part: part[position], pieces))
        return jax.tree.map(lambda new, old: jnp.where(position < mine, new, old), longer, subtotal)

    return lax.fori_loop(0, count - 1, hop, subtotal)


def block_local(log_step, cutoff, write_mat, read_mat, scaled, grad_out):
    length, head_count = log_step.shape
    group_size = min(8, head_count)
    group_count = head_count // group_size
    cumlog = jnp.cumsum(log_step, axis=0)
    segment = jnp.cumsum(cutoff)
    places = jnp.arange(length)
    causal = (places[:, None] >= places[None, :]) & (segment[:, None] == segment[None, :])
    scores = jnp.dot(read_mat, write_mat.T, preferred_element_type=jnp.float32)
    out_list = []
    back_list = []
    dcum_list = []
    weighted_sum = jnp.zeros((length, length), jnp.float32)
    for group in range(group_count):
        lower = group * group_size
        upper = lower + group_size
        cum_part = cumlog[:, lower:upper].T
        scaled_part = scaled[:, lower:upper, :]
        grad_part = grad_out[:, lower:upper, :]
        decays = jnp.exp(
            jnp.where(causal[None], cum_part[:, :, None] - cum_part[:, None, :], -jnp.inf)
        )
        weights = (scores[None] * decays).astype(jnp.bfloat16)
        out_list.append(
            jnp.einsum("gts,sgp->tgp", weights, scaled_part, preferred_element_type=jnp.float32)
        )
        back_list.append(
            jnp.einsum("gts,tgp->sgp", weights, grad_part, preferred_element_type=jnp.float32)
        )
        pair_dot = jnp.einsum(
            "tgp,sgp->gts", grad_part, scaled_part, preferred_element_type=jnp.float32
        )
        weighted = decays * pair_dot
        kernel = scores[None] * weighted
        weighted_sum = weighted_sum + jnp.sum(weighted, axis=0)
        dcum_list.append(jnp.sum(kernel, axis=2) - jnp.sum(kernel, axis=1))
    intra_out = jnp.concatenate(out_list, axis=1)
    intra_back = jnp.concatenate(back_list, axis=1)
    dcum = jnp.concatenate(dcum_list, axis=0).T
    local_grad = jnp.flip(jnp.cumsum(jnp.flip(dcum, 0), axis=0), 0)
    to_end = (
        jnp.exp(cumlog[-1][None, :] - cumlog)
        * (segment[-1] == segment).astype(jnp.float32)[:, None]
    )
    from_start = jnp.exp(cumlog) * (segment == 0).astype(jnp.float32)[:, None]
    chain_total = jnp.exp(cumlog[-1]) * (segment[-1] == 0).astype(jnp.float32)
    end_scaled = to_end[:, :, None] * scaled
    start_grad = from_start[:, :, None] * grad_out
    carry_state = jnp.einsum(
        "sn,shp->hnp", write_mat, end_scaled, precision=PRECISE, preferred_element_type=jnp.float32
    )
    adjoint_state = jnp.einsum(
        "tn,thp->hnp", read_mat, start_grad, precision=PRECISE, preferred_element_type=jnp.float32
    )
    return (
        intra_out,
        intra_back,
        local_grad,
        weighted_sum,
        chain_total,
        from_start,
        to_end,
        end_scaled,
        start_grad,
        carry_state,
        adjoint_state,
    )


def block_finish(pieces, scaled, grad_out, write_mat, read_mat, carry_in, adjoint_in):
    (
        intra_out,
        intra_back,
        local_grad,
        weighted_sum,
        chain_total,
        from_start,
        to_end,
        end_scaled,
        start_grad,
    ) = pieces[:9]
    across_out = from_start[:, :, None] * jnp.einsum(
        "tn,hnp->thp", read_mat, carry_in, precision=PRECISE, preferred_element_type=jnp.float32
    )
    across_back = to_end[:, :, None] * jnp.einsum(
        "sn,hnp->shp", write_mat, adjoint_in, precision=PRECISE, preferred_element_type=jnp.float32
    )
    grad_read = jnp.dot(
        weighted_sum, write_mat, precision=PRECISE, preferred_element_type=jnp.float32
    ) + jnp.einsum("hnp,thp->tn", carry_in, start_grad, precision=PRECISE)
    grad_write = jnp.dot(
        weighted_sum.T, read_mat, precision=PRECISE, preferred_element_type=jnp.float32
    ) + jnp.einsum("hnp,shp->sn", adjoint_in, end_scaled, precision=PRECISE)
    inflow = jnp.sum(across_out * grad_out, axis=2)
    outflow = jnp.sum(across_back * scaled, axis=2)
    log_grads = (
        local_grad
        + jnp.flip(jnp.cumsum(jnp.flip(inflow, 0), axis=0), 0)
        + jnp.cumsum(outflow, axis=0)
        - outflow
    )
    log_grads = (
        log_grads + chain_total[None, :] * jnp.sum(carry_in * adjoint_in, axis=(1, 2))[None, :]
    )
    return (intra_out + across_out, intra_back + across_back, grad_read, grad_write, log_grads)


def combine_link(earlier, later):
    return (earlier[0] * later[0], later[1] + later[0][:, None] * earlier[1])


def local(inputs, step_sizes, write_vecs, read_vecs, log_rates, skip_gain, resets, cotangent):
    tokens = inputs.shape[1]
    head_count = step_sizes.shape[2]
    head_width = inputs.shape[2] // head_count
    state_width = write_vecs.shape[2]
    features = inputs[0].reshape(tokens, head_count, head_width)
    grad_out = cotangent[0].reshape(tokens, head_count, head_width)
    deltas = step_sizes[0]
    write_mat = write_vecs[0]
    read_mat = read_vecs[0]
    decay_rates = jnp.exp(log_rates)
    scaled = (deltas[:, :, None] * features).astype(jnp.bfloat16)
    log_step = -deltas * decay_rates[None, :]
    places = lax.axis_index("seq") * tokens + jnp.arange(tokens, dtype=jnp.int32)
    reset_marks = resets[0]
    cut_here = jnp.any(places[:, None] == reset_marks[None, :], axis=1).astype(jnp.float32)
    cut_next = jnp.any(places[:, None] + 1 == reset_marks[None, :], axis=1).astype(jnp.float32)
    forward_pieces = block_local(log_step, cut_here, write_mat, read_mat, scaled, grad_out)
    flipped = tuple(
        (jnp.flip(a, 0) for a in (log_step, cut_next, write_mat, read_mat, scaled, grad_out))
    )
    reverse_pieces = block_local(
        flipped[0], flipped[1], flipped[2], flipped[3], flipped[4], flipped[5]
    )
    flat_width = state_width * head_width
    state_shape = (head_count, state_width, head_width)
    unit = jnp.ones((head_count,), jnp.float32)
    empty = jnp.zeros((head_count, flat_width), jnp.float32)
    fwd_carry = forward_pieces[9].reshape(head_count, flat_width)
    fwd_adjoint = forward_pieces[10].reshape(head_count, flat_width)
    rev_carry = reverse_pieces[9].reshape(head_count, flat_width)
    rev_adjoint = reverse_pieces[10].reshape(head_count, flat_width)
    fwd_total = forward_pieces[4]
    rev_total = reverse_pieces[4]
    fwd_in = prefix((fwd_total, fwd_carry), "seq", combine_link, (unit, empty), False)[1]
    fwd_adj_in = prefix((fwd_total, fwd_adjoint), "seq", combine_link, (unit, empty), True)[1]
    rev_in = prefix((rev_total, rev_carry), "seq", combine_link, (unit, empty), True)[1]
    rev_adj_in = prefix((rev_total, rev_adjoint), "seq", combine_link, (unit, empty), False)[1]
    fwd_mixed, fwd_back, fwd_read, fwd_write, fwd_log = block_finish(
        forward_pieces,
        scaled,
        grad_out,
        write_mat,
        read_mat,
        fwd_in.reshape(state_shape),
        fwd_adj_in.reshape(state_shape),
    )
    rev_results = block_finish(
        reverse_pieces,
        flipped[4],
        flipped[5],
        flipped[2],
        flipped[3],
        rev_in.reshape(state_shape),
        rev_adj_in.reshape(state_shape),
    )
    rev_mixed, rev_back, rev_read, rev_write, rev_log = tuple((jnp.flip(a, 0) for a in rev_results))
    grad_scaled = fwd_back + rev_back
    log_total = fwd_log + rev_log
    mixed = fwd_mixed + rev_mixed + skip_gain[None, :, None] * features
    outputs = mixed.astype(jnp.bfloat16).reshape(1, tokens, head_count * head_width)
    grad_in = deltas[:, :, None] * grad_scaled + skip_gain[None, :, None] * grad_out
    grad_inputs = grad_in.astype(jnp.bfloat16).reshape(1, tokens, head_count * head_width)
    grad_steps = (jnp.sum(features * grad_scaled, axis=2) - decay_rates[None, :] * log_total)[None]
    grad_write = (fwd_write + rev_write)[None]
    grad_read = (fwd_read + rev_read)[None]
    rate_part = -jnp.sum(decay_rates[None, :] * deltas * log_total, axis=0)
    skip_part = jnp.sum(features.astype(jnp.float32) * grad_out.astype(jnp.float32), axis=(0, 2))
    grad_rates, grad_skip = lax.psum((rate_part, skip_part), ("seq", "dp"))
    return (outputs, grad_inputs, grad_steps, grad_write, grad_read, grad_rates, grad_skip)


def solution(mesh):
    in_specs = (
        P("dp", "seq", None),
        P("dp", "seq", None),
        P("dp", "seq", None),
        P("dp", "seq", None),
        P(),
        P(),
        P("dp", None),
        P("dp", "seq", None),
    )
    out_specs = (
        P("dp", "seq", None),
        P("dp", "seq", None),
        P("dp", "seq", None),
        P("dp", "seq", None),
        P("dp", "seq", None),
        P(),
        P(),
    )
    return jax.shard_map(local, mesh=mesh, in_specs=in_specs, out_specs=out_specs, check_vma=False)
```

profile of v0, /device:TPU:0, one launch (start us, length us, event | category | flops | bytes accessed | tf_op | source)
XLA Modules:
  0.0 432.8 jit_solution(11219131024639504343)
XLA Ops:
  26.5 2.5 copy.239
  29.0 2.4 all_gather_reshape.14
  33.0 2.5 copy.213
  35.5 2.4 all_gather_reshape.12
  43.5 23.1 %all-gather = f32[16,1,32]{2,1,0:T(1,128)S(1)} all-gather(f32[1,1,32]{2,1,0:T(1,128)} %get-tuple-element.610), channel_id=1, replica_groups=mesh['seq'=16,'dp'=2] {'seq'}, dimensions={0}, use_global_device_ids=true | all-gather | bytes 2176 | tf_op jit(solution)/shard_map/all_gather | solution.py:11
  67.2 17.9 %all-gather.1 = f32[16,1,32]{2,1,0:T(1,128)S(1)} all-gather(f32[1,1,32]{2,1,0:T(1,128)} %get-tuple-element.606), channel_id=1, replica_groups=mesh['seq'=16,'dp'=2] {'seq'}, dimensions={0}, use_global_device_ids=true | all-gather | bytes 2176 | tf_op jit(solution)/shard_map/all_gather | solution.py:11
  121.8 28.3 %while.59 = (s32[]{:T(128)}, f32[32,4096]{1,0:T(8,128)S(1)}, s32[]{:T(128)}, f32[16,32,4096]{2,1,0:T(8,128)}, f32[16,32]{1,0:T(8,128)}, /*index=5*/s32[]{:T(128)}, s32[]{:T(128)}) while((s32[]{:T(128)}, f32[32,4096]{1,0:T(8,128)S(1)}, s32[]{:T(128)}, f32[16,32,4096]{2,1,0:T(8,128)}, f32[16,32]{1,0:T(8,128)}, ...), condition=%wide.region_13.14_spmd.clone, body=%wide.region_12.13_spmd.clone.sunk | while | flops 524292 | bytes 1573361 | solution.py:23
  151.4 3.6 maximum_add_fusion.3
  157.3 14.2 %all-gather.11.cloned.1.call-done = f32[16,32,4096]{2,1,0:T(8,128)} async-done(((f32[1,32,4096]{2,1,0:T(8,128)}), f32[16,32,4096]{2,1,0:T(8,128)}) %all-gather.11.cloned.1.call-update) | async-done | bytes 8388624 | tf_op jit(solution)/shard_map/all_gather | solution.py:11
  171.5 7.6 %rev.83 = f32[16,32,4096]{2,1,0:T(8,128)} reverse(f32[16,32,4096]{2,1,0:T(8,128)} %all-gather.11.cloned.1.call-done), dimensions={0} | reverse | bytes 16777216 | tf_op jit(solution)/shard_map/rev | solution.py:13
  179.1 28.3 %while.58 = (s32[]{:T(128)}, f32[32,4096]{1,0:T(8,128)S(1)}, s32[]{:T(128)}, f32[16,32,4096]{2,1,0:T(8,128)}, f32[16,32]{1,0:T(8,128)}, /*index=5*/s32[]{:T(128)}, s32[]{:T(128)}) while((s32[]{:T(128)}, f32[32,4096]{1,0:T(8,128)S(1)}, s32[]{:T(128)}, f32[16,32,4096]{2,1,0:T(8,128)}, f32[16,32]{1,0:T(8,128)}, ...), condition=%wide.region_11.12_spmd.clone, body=%wide.region_10.11_spmd.clone.sunk | while | flops 524292 | bytes 1573361 | solution.py:23
  208.9 4.3 multiply_reduce_fusion
  215.2 2.5 convolution_bitcast_fusion.5
  217.6 2.5 copy.231
  220.2 2.4 all_gather_reshape.13
  222.6 24.3 %all-gather.7.cloned.1.call-done = f32[16,32,4096]{2,1,0:T(8,128)} async-done(((f32[1,32,4096]{2,1,0:T(8,128)}), f32[16,32,4096]{2,1,0:T(8,128)}) %all-gather.7.cloned.1.call-update) | async-done | bytes 8388624 | tf_op jit(solution)/shard_map/all_gather | solution.py:11
  246.9 28.5 %while.56 = (s32[]{:T(128)}, f32[32,4096]{1,0:T(8,128)S(1)}, s32[]{:T(128)}, f32[16,32,4096]{2,1,0:T(8,128)}, f32[16,32]{1,0:T(8,128)}, /*index=5*/s32[]{:T(128)}, s32[]{:T(128)}) while((s32[]{:T(128)}, f32[32,4096]{1,0:T(8,128)S(1)}, s32[]{:T(128)}, f32[16,32,4096]{2,1,0:T(8,128)}, f32[16,32]{1,0:T(8,128)}, /*index=5*/s32[]{:T(128)}, ...), condition=%wide.region_4.5_spmd.clone, body=%wide.region_3.4_spmd.clone.sunk | while | flops 524292 | bytes 1573361 | solution.py:23
  282.2 2.6 multiply_reduce_fusion.12
  299.7 2.7 multiply_reduce_fusion.4
  319.4 2.8 convolution_bitcast_fusion.32
  335.0 7.6 %rev.80 = f32[16,32,4096]{2,1,0:T(8,128)} reverse(f32[16,32,4096]{2,1,0:T(8,128)} %all-gather.9.cloned.1.call-done), dimensions={0} | reverse | bytes 16777216 | tf_op jit(solution)/shard_map/rev | solution.py:13
  342.6 28.4 %while.57 = (s32[]{:T(128)}, f32[32,4096]{1,0:T(8,128)S(1)}, s32[]{:T(128)}, f32[16,32,4096]{2,1,0:T(8,128)}, f32[16,32]{1,0:T(8,128)}, /*index=5*/s32[]{:T(128)}, s32[]{:T(128)}) while((s32[]{:T(128)}, f32[32,4096]{1,0:T(8,128)S(1)}, s32[]{:T(128)}, f32[16,32,4096]{2,1,0:T(8,128)}, f32[16,32]{1,0:T(8,128)}, /*index=5*/s32[]{:T(128)}, ...), condition=%wide.region_9.10_spmd.clone, body=%wide.region_8.9_spmd.clone.sunk | while | flops 524292 | bytes 1573361 | solution.py:23
  379.3 2.7 fusion.29
  387.4 38.9 %all-reduce = (f32[32]{0:T(128)}, f32[32]{0:T(128)}) all-reduce(f32[32]{0:T(128)S(1)} %neg.7, f32[32]{0:T(128)} %reduce_sum.344), channel_id=1, replica_groups=mesh['seq'=16,'dp'=2] {'seq','dp'}, use_global_device_ids=true, to_apply=%region_52.53 | all-reduce | flops 64 | bytes 512 | tf_op jit(solution)/shard_map/psum | solution.py:205
  (353 shorter events, 245.7 us)
Async XLA Ops:
  7.2 17.8 %copy-start.7 = (bf16[1,128,64]{1,2,0:T(8,128)(2,1)S(1)}, bf16[1,128,64]{1,2,0:T(8,128)(2,1)}, u32[]{:S(2)}) copy-start(bf16[1,128,64]{1,2,0:T(8,128)(2,1)} %param.19) | copy-start | bytes 49156
  7.2 114.6 %all-gather.13.cloned.1.call-start = ((), (), s32[]{:S(2)}) async-start(), calls=%async_computation.3 | async-start | bytes 8912896 | tf_op jit(solution)/shard_map/all_gather | solution.py:11
  18.3 153.2 %all-gather.11.cloned.1.call-start = ((), (), s32[]{:S(2)}) async-start(), calls=%async_computation.2 | async-start | bytes 8912896 | tf_op jit(solution)/shard_map/all_gather | solution.py:11
  23.0 18.8 %copy-start.2 = (bf16[1,128,2048]{1,2,0:T(8,128)(2,1)}, bf16[1,128,2048]{1,2,0:T(8,128)(2,1)S(1)}, u32[]{:S(2)}) copy-start(bf16[1,128,2048]{1,2,0:T(8,128)(2,1)S(1)} %copy.196) | copy-start | bytes 1572868
  23.9 17.1 %copy-start.1 = (f32[1,128,2048]{1,2,0:T(8,128)}, f32[1,128,2048]{1,2,0:T(8,128)S(1)}, u32[]{:S(2)}) copy-start(f32[1,128,2048]{1,2,0:T(8,128)S(1)} %get-tuple-element.585) | copy-start | bytes 3145732
  31.5 215.4 %all-gather.7.cloned.1.call-start = ((), (), s32[]{:S(2)}) async-start(), calls=%async_computation | async-start | bytes 8912896 | tf_op jit(solution)/shard_map/all_gather | solution.py:11
  38.0 297.1 %all-gather.9.cloned.1.call-start = ((), (), s32[]{:S(2)}) async-start(), calls=%async_computation.1 | async-start | bytes 8912896 | tf_op jit(solution)/shard_map/all_gather | solution.py:11
  42.6 172.5 %copy-start.6 = (bf16[128,64]{0,1:T(8,128)(2,1)}, bf16[128,64]{0,1:T(8,128)(2,1)S(1)}, u32[]{:S(2)}) copy-start(bf16[128,64]{0,1:T(8,128)(2,1)S(1)} %rev.76) | copy-start | bytes 49156
  66.6 19.2 %copy-start.18 = (f32[16,1,32]{2,1,0:T(1,128)}, f32[16,1,32]{2,1,0:T(1,128)S(1)}, u32[]{:S(2)}) copy-start(f32[16,1,32]{2,1,0:T(1,128)S(1)} %all-gather) | copy-start | bytes 6148
  86.6 128.5 %copy-start.10 = (f32[128,32]{0,1:T(8,128)}, f32[128,32]{0,1:T(8,128)S(1)}, u32[]{:S(2)}) copy-start(f32[128,32]{0,1:T(8,128)S(1)} %copy.230) | copy-start | bytes 49156
  179.1 29.8 %copy-start.15 = (f32[128,32]{0,1:T(8,128)S(1)}, f32[128,32]{0,1:T(8,128)}, u32[]{:S(2)}) copy-start(f32[128,32]{0,1:T(8,128)} %copy-done.14) | copy-start | bytes 49156
  179.1 29.8 %copy-start.32 = (f32[32]{0:T(128)S(1)}, f32[32]{0:T(128)}, u32[]{:S(2)}) copy-start(f32[32]{0:T(128)} %param.21) | copy-start | bytes 388
  213.2 65.2 %copy-start.20 = (pred[128,128]{0,1:T(8,128)(4,1)S(1)}, pred[128,128]{0,1:T(8,128)(4,1)}, u32[]{:S(2)}) copy-start(pred[128,128]{0,1:T(8,128)(4,1)} %fusion.123) | copy-start | bytes 49156
  213.2 65.2 %copy-start.25 = (f32[8,128]{1,0:T(8,128)S(1)}, f32[8,128]{1,0:T(8,128)}, u32[]{:S(2)}) copy-start(f32[8,128]{1,0:T(8,128)} %copy.199) | copy-start | bytes 12292
  220.2 60.7 %copy-start.29 = (f32[8,128]{1,0:T(8,128)S(1)}, f32[8,128]{1,0:T(8,128)}, u32[]{:S(2)}) copy-start(f32[8,128]{1,0:T(8,128)} %copy.205) | copy-start | bytes 12292
  222.6 59.6 %copy-start.16 = (f32[128,128]{0,1:T(8,128)S(1)}, f32[128,128]{0,1:T(8,128)}, u32[]{:S(2)}) copy-start(f32[128,128]{0,1:T(8,128)} %fusion.135) | copy-start | bytes 196612
  222.6 59.6 %copy-start.27 = (f32[8,128]{1,0:T(8,128)S(1)}, f32[8,128]{1,0:T(8,128)}, u32[]{:S(2)}) copy-start(f32[8,128]{1,0:T(8,128)} %copy.208) | copy-start | bytes 12292
  288.4 17.9 %copy-start.11 = (f32[128,32]{0,1:T(8,128)S(1)}, f32[128,32]{0,1:T(8,128)}, u32[]{:S(2)}) copy-start(f32[128,32]{0,1:T(8,128)} %copy-done.10) | copy-start | bytes 49156
  313.7 17.1 %copy-start.17 = (f32[128,128]{0,1:T(8,128)S(1)}, f32[128,128]{0,1:T(8,128)}, u32[]{:S(2)}) copy-start(f32[128,128]{0,1:T(8,128)} %fusion.135) | copy-start | bytes 196612
  313.7 17.1 %copy-start.21 = (pred[128,128]{0,1:T(8,128)(4,1)S(1)}, pred[128,128]{0,1:T(8,128)(4,1)}, u32[]{:S(2)}) copy-start(pred[128,128]{0,1:T(8,128)(4,1)} %fusion.123) | copy-start | bytes 49156
  313.7 17.1 %copy-start.28 = (f32[8,128]{1,0:T(8,128)S(1)}, f32[8,128]{1,0:T(8,128)}, u32[]{:S(2)}) copy-start(f32[8,128]{1,0:T(8,128)} %copy.208) | copy-start | bytes 12292
  313.8 18.1 %copy-start.30 = (f32[8,128]{1,0:T(8,128)S(1)}, f32[8,128]{1,0:T(8,128)}, u32[]{:S(2)}) copy-start(f32[8,128]{1,0:T(8,128)} %copy.205) | copy-start | bytes 12292
  313.8 19.2 %copy-start.31 = (f32[8,128]{1,0:T(8,128)S(1)}, f32[8,128]{1,0:T(8,128)}, u32[]{:S(2)}) copy-start(f32[8,128]{1,0:T(8,128)} %copy.202) | copy-start | bytes 12292
  313.8 20.2 %copy-start.26 = (f32[8,128]{1,0:T(8,128)S(1)}, f32[8,128]{1,0:T(8,128)}, u32[]{:S(2)}) copy-start(f32[8,128]{1,0:T(8,128)} %copy.199) | copy-start | bytes 12292
  (13 other events, 135.1 us)
Sparse Core Ops, SparseCore 0:
  18.5 77.6 all-gather.12
  98.3 73.1 all-gather.10
  173.7 73.1 all-gather.6
  248.9 73.1 all-gather.8
where the time goes:
time: 440 us; the launch traced here: 433 us
  local copies, waits for them, and re-layouts  132 us (30%)
  other arithmetic  90.6 us (21%)
  blocking collectives  79.9 us (18%)
  matrix products  74.5 us (17%)
  waiting for transfers between devices  38.5 us (9%)
  between operations  15.6 us (4%)
    select_n x60, other arithmetic, hop(): jnp.where(position < mine, new, old)  70.2 us
    mul x60, local copies, waits for them, and re-layouts, combine_link(): return (earlier[0] * later[0], later[1] + later[0][:, None] * earlier[1])  41.3 us
    all_gather x2, blocking collectives, prefix(): pieces = jax.tree.map(lambda part: lax.all_gather(part, axis), value)  41 us
    psum x1, blocking collectives, local(): grad_rates, grad_skip = lax.psum((rate_part, skip_part), ('seq', 'dp'))  38.9 us
    all_gather x4, waiting for transfers between devices, prefix(): pieces = jax.tree.map(lambda part: lax.all_gather(part, axis), value)  38.4 us
    rev x4, local copies, waits for them, and re-layouts, prefix(): pieces = jax.tree.map(lambda part: part[::-1], pieces)  16.4 us
    dot_general x8, matrix products, block_local(): jnp.einsum('gts,tgp->sgp', weights, grad_part, preferred_element_type=jnp...  15.9 us
    transpose x10, local copies, waits for them, and re-layouts, block_local(): cum_part = cumlog[:, lower:upper].T  13.5 us
  transfers between devices with their start and end apart: 4, of which 2 were waited for; matrix products, arithmetic and copies ran while one was open for 54% of the time, Pallas kernels for 0%

commit v1 on v0

v1 whole, which is shorter than its diff:
```python
import functools
import math

import jax
import jax.numpy as jnp
from jax import lax
from jax.experimental import pallas as pl
from jax.experimental.pallas import tpu as pltpu
from jax.sharding import PartitionSpec as P

F32 = jnp.float32
BF16 = jnp.bfloat16
LANES = 128
WIDE = 256
CHUNKS = 4
NN = (((1,), (0,)), ((), ()))
NT = (((1,), (1,)), ((), ()))
TN = (((0,), (0,)), ((), ()))


def mm(a, b, dims=NN):
    return lax.dot_general(a, b, dims, preferred_element_type=F32)


def exact(a, b):
    return jnp.dot(a, b, precision=lax.Precision.HIGHEST, preferred_element_type=F32)


def halves(value):
    upper = value.astype(BF16)
    return upper, (value - upper.astype(F32)).astype(BF16)


def thirds(value):
    upper = value.astype(BF16)
    rest = value - upper.astype(F32)
    middle = rest.astype(BF16)
    return upper, middle, (rest - middle.astype(F32)).astype(BF16)


def iota(shape, dim):
    return lax.broadcasted_iota(jnp.int32, shape, dim)


def block_tables(deltas, log_rates, resets_ref, first):
    length = deltas.shape[0]
    square = (length, length)
    row, col = iota(square, 0), iota(square, 1)
    lower = (row >= col).astype(F32)
    upper = (row <= col).astype(F32)
    rates = jnp.exp(log_rates)
    lam = -deltas * rates
    cum = exact(lower, lam)

    def marks(grid, ahead):
        hit = jnp.zeros(square, jnp.bool_)
        for k in range(resets_ref.shape[1]):
            hit = hit | (grid + (first + ahead) == resets_ref[0, k])
        return hit.astype(BF16)

    low16, up16 = lower.astype(BF16), upper.astype(BF16)
    seg_f = mm(low16, marks(row, 0)), mm(marks(col, 0), up16)
    seg_r = mm(up16, marks(row, 1)), mm(marks(col, 1), low16)
    return rates, lam, cum, lower, upper, seg_f, seg_r


def expander(heads, width, start):
    shape = (3 * heads, width)
    per_head = 2 * LANES // 4
    return (iota(shape, 0) % heads == (iota(shape, 1) + start) // per_head).astype(BF16)


def spread_parts(values):
    return jnp.concatenate([jnp.concatenate(thirds(v), axis=1) for v in values], axis=0)


def factors(deltas, lam, cum):
    before = cum - lam
    return [deltas, jnp.exp(cum), jnp.exp(-cum), jnp.exp(-before), jnp.exp(before)]


def place_of(start, parts, chips):
    part, chip = divmod(start // WIDE, chips)
    return part // parts, part % parts, chip


def totals_kernel(deltas_ref, rates_ref, resets_ref, out_ref):
    deltas = deltas_ref[...]
    length, heads = deltas.shape
    first = lax.axis_index("seq") * length
    chain = jnp.exp(-jnp.exp(rates_ref[...]) * jnp.sum(deltas, axis=0, keepdims=True))
    clear_f, clear_r = jnp.float32(1.0), jnp.float32(1.0)
    for k in range(resets_ref.shape[1]):
        at = resets_ref[0, k] - first
        clear_f = jnp.where((at >= 0) & (at < length), 0.0, clear_f)
        clear_r = jnp.where((at >= 1) & (at < length + 1), 0.0, clear_r)
    out_ref[0:1, 0:heads] = chain * clear_f
    out_ref[0:1, heads : 2 * heads] = chain * clear_r


def states_kernel(chunks, chips, x_ref, cot_ref, deltas_ref, write_ref, read_ref, rates_ref, resets_ref, *outs):
    length, channels = x_ref.shape
    heads = deltas_ref.shape[1]
    index = lax.axis_index("seq")
    core = lax.rem(index, 2)
    deltas = deltas_ref[...]
    rates, lam, cum, lower, upper, seg_f, seg_r = block_tables(deltas, rates_ref[...], resets_ref, index * length)
    states = write_ref.shape[1]
    seg_fc, seg_rc = seg_f[0][:, :states], seg_r[0][:, :states]
    write, read = write_ref[...], read_ref[...]
    zero = jnp.zeros_like(write)
    write_f = jnp.where(seg_fc == seg_fc[length - 1 : length], write, zero)
    write_r = jnp.where(seg_rc == seg_rc[0:1], write, zero)
    read_f = jnp.where(seg_fc == 0.0, read, zero)
    read_r = jnp.where(seg_rc == 0.0, read, zero)
    parts = spread_parts(factors(deltas, lam, cum))
    keep, send = outs[:chunks], outs[chunks:]
    for start in range(0, channels, WIDE):
        spread = mm(parts, expander(heads, WIDE, start))
        step, u_f, v_f, u_r, v_r = (spread[i * length : (i + 1) * length] for i in range(5))
        lanes = slice(start, start + WIDE)
        scaled = (step * x_ref[:, lanes].astype(F32)).astype(BF16).astype(F32)
        cot = cot_ref[:, lanes].astype(F32)
        chain = u_f[length - 1 : length]
        carry_f = mm(write_f, (v_f * scaled).astype(BF16), TN) * chain
        carry_r = mm(write_r, (v_r * scaled).astype(BF16), TN)
        adj_f = mm(read_f, (u_f * cot).astype(BF16), TN)
        adj_r = mm(read_r, (u_r * cot).astype(BF16), TN) * chain
        chunk, part, chip = place_of(start, keep[0].shape[2], chips)
        for scan, value in enumerate((carry_f, adj_r, adj_f, carry_r)):
            zeroth, other = value[:, :LANES], value[:, LANES:]
            keep[chunk][scan, chip, part] = jnp.where(core == 0, zeroth, other)
            send[chunk][scan, chip, part] = jnp.where(core == 0, other, zeroth)


class Chain:
    def __init__(self, table_ref, heads, index, chips):
        self.table, self.heads, self.index, self.chips = table_ref, heads, index, chips

    def block(self, device, scan, pair):
        row = jnp.bitwise_xor(self.index, device)
        base = (scan % 2) * self.heads + 2 * pair
        return self.table[row, base], self.table[row, base + 1]

    def over(self, first, count, scan, pair):
        low, high = jnp.float32(1.0), jnp.float32(1.0)
        for k in range(count):
            a, b = self.block(first + k, scan, pair)
            low, high = low * a, high * b
        return low, high


def lanes_of(pair):
    lane = iota((1, LANES), 1)
    return jnp.where(lane < LANES // 2, pair[0], pair[1])


def mul2(a, b):
    return a[0] * b[0], a[1] * b[1]


def pick2(cond, a, b):
    return jnp.where(cond, a[0], b[0]), jnp.where(cond, a[1], b[1])


ONE2 = (1.0, 1.0)


def position(chips):
    index = lax.axis_index("seq")
    core = lax.rem(index, 2)
    chip = lax.rem(lax.div(index, 2), chips)
    return index, core, chip


def pair_number(part, chips, chip, core):
    return (part * chips + chip) * 2 + core


def chip_kernel(chunk, chips, heads, table_ref, keep_ref, got_ref, *outs):
    index, core, chip = position(chips)
    base = index - core
    chain = Chain(table_ref, heads, index, chips)
    parts = keep_ref.shape[2]
    for shift in range(chips):
        owner = lax.rem(chip + shift, chips)
        for part in range(parts):
            pair = pair_number(chunk * parts + part, chips, owner, core)
            for scan in range(4):
                mine, other = keep_ref[scan, owner, part], got_ref[scan, owner, part]
                if scan < 2:
                    factor = chain.block(base + 1, scan, pair)
                    a, b = pick2(core == 0, factor, ONE2), pick2(core == 0, ONE2, factor)
                else:
                    factor = chain.block(base, scan, pair)
                    a, b = pick2(core == 0, ONE2, factor), pick2(core == 0, factor, ONE2)
                outs[shift][scan, part] = lanes_of(a) * mine + lanes_of(b) * other


def plane_kernel(chunk, chips, heads, table_ref, *refs):
    gathered, (out_ref,) = refs[:chips], refs[chips:]
    index, core, chip = position(chips)
    base = index - core - 2 * chip
    chain = Chain(table_ref, heads, index, chips)
    parts = out_ref.shape[1]
    for part in range(parts):
        pair = pair_number(chunk * parts + part, chips, chip, core)
        for scan in range(4):
            whole = [chain.over(base + 2 * other, 2, scan, pair) for other in range(chips)]
            total = None
            for shift in range(chips):
                place = lax.rem(chip + shift, chips)
                weight = ONE2
                for other in range(chips):
                    beyond = other > place if scan < 2 else other < place
                    weight = mul2(weight, pick2(beyond, whole[other], ONE2))
                term = lanes_of(weight) * gathered[shift][scan, part]
                total = term if total is None else total + term
            out_ref[scan, part] = total


def joined(level, chips, chain, plane, scan, pair, entered, got):
    bit = lax.rem(lax.shift_right_logical(plane, level), 2)
    first = plane - lax.rem(plane, 2**level)
    takes = bit == 1 if scan < 2 else bit == 0
    weight = pick2(takes, ONE2, (0.0, 0.0))
    if level > 0:
        for k in range(2**level):
            between = first + k < plane if scan < 2 else first + k > plane
            weight = mul2(weight, pick2(between, chain.over((first + k) * 2 * chips, 2 * chips, scan, pair), ONE2))
    value = lanes_of(weight) * got
    return value if entered is None else entered + value


def hop_kernel(chunk, chips, heads, level, last, table_ref, *refs):
    (entered_ref, refs) = (refs[0], refs[1:]) if level > 0 else (None, refs)
    total_ref, got_ref, new_ref, onward_ref = refs
    index, core, chip = position(chips)
    plane = lax.div(index, 2 * chips)
    chain = Chain(table_ref, heads, index, chips)
    parts = got_ref.shape[1]
    size = 2**level
    bit = lax.rem(lax.shift_right_logical(plane, level), 2)
    after = lax.rem(lax.shift_right_logical(plane, level + 1), 2)
    mine = plane - lax.rem(plane, size)
    far = jnp.bitwise_xor(mine, size)
    for part in range(parts):
        pair = pair_number(chunk * parts + part, chips, chip, core)
        totals = []
        for scan in range(4):
            got, own = got_ref[scan, part], total_ref[scan, part]
            entered = entered_ref[scan, part] if level > 0 else None
            new_ref[scan, part] = joined(level, chips, chain, plane, scan, pair, entered, got)
            near_factor = chain.over(mine * 2 * chips, 2 * chips * size, scan, pair)
            far_factor = chain.over(far * 2 * chips, 2 * chips * size, scan, pair)
            later = bit == 1 if scan < 2 else bit == 0
            a, b = pick2(later, ONE2, far_factor), pick2(later, near_factor, ONE2)
            totals.append(lanes_of(a) * own + lanes_of(b) * got)
        if last:
            for scan in range(2):
                onward_ref[scan, part] = jnp.where(after == 0, totals[scan], totals[scan + 2])
        else:
            for scan in range(4):
                onward_ref[scan, part] = totals[scan]


def spread_kernel(chunk, chips, heads, level, table_ref, entered_ref, got_ref, *refs):
    gathered, outs = refs[:chips], refs[chips:]
    index, core, chip = position(chips)
    plane = lax.div(index, 2 * chips)
    chain = Chain(table_ref, heads, index, chips)
    parts = got_ref.shape[1]
    base = plane * 2 * chips
    for part in range(parts):
        pair = pair_number(chunk * parts + part, chips, chip, core)
        for scan in range(4):
            value = joined(level, chips, chain, plane, scan, pair, entered_ref[scan, part], got_ref[scan % 2, part])
            whole = [chain.over(base + 2 * other, 2, scan, pair) for other in range(chips)]
            for shift in range(chips):
                target = lax.rem(chip + shift, chips)
                weight = ONE2
                for other in range(chips):
                    ahead = other < target if scan < 2 else other > target
                    weight = mul2(weight, pick2(ahead, whole[other], ONE2))
                total = lanes_of(weight) * value
                for source in range(chips):
                    if source == shift:
                        continue
                    place = lax.rem(chip + source, chips)
                    counts = place < target if scan < 2 else place > target
                    weight = pick2(counts, ONE2, (0.0, 0.0))
                    for other in range(chips if chips > 2 else 0):
                        if scan < 2:
                            between = (other > place) & (other < target)
                        else:
                            between = (other < place) & (other > target)
                        weight = mul2(weight, pick2(between, whole[other], ONE2))
                    total = total + lanes_of(weight) * gathered[source][scan, part]
                outs[shift][scan, part] = total


def core_kernel(chunk, chips, heads, table_ref, keep_ref, got_ref, *refs):
    entered, (own_ref, send_ref) = refs[:chips], refs[chips:]
    index, core, chip = position(chips)
    chain = Chain(table_ref, heads, index, chips)
    parts = keep_ref.shape[2]
    for shift in range(chips):
        owner = lax.rem(chip + chips - shift, chips)
        for part in range(parts):
            pair = pair_number(chunk * parts + part, chips, owner, core)
            for scan in range(4):
                value = entered[shift][scan, part]
                mine, other = keep_ref[scan, owner, part], got_ref[scan, owner, part]
                near = core == 0 if scan < 2 else core == 1
                to_own = lanes_of(chain.block(jnp.bitwise_xor(index, 1), scan, pair)) * value + other
                to_other = lanes_of(chain.block(index, scan, pair)) * value + mine
                own_ref[scan, owner, part] = jnp.where(near, value, to_own)
                send_ref[scan, owner, part] = jnp.where(near, to_other, value)


def finish_kernel(chunks, chips, x_ref, cot_ref, deltas_ref, write_ref, read_ref, rates_ref, skip_ref, resets_ref, *refs):
    own, got = refs[:chunks], refs[chunks : 2 * chunks]
    out_ref, gin_ref, steps_ref, gwrite_ref, gread_ref, small_ref = refs[2 * chunks :]
    length, channels = x_ref.shape
    heads = deltas_ref.shape[1]
    states = write_ref.shape[1]
    index = lax.axis_index("seq")
    core = lax.rem(index, 2)
    deltas = deltas_ref[...]
    rates, lam, cum, lower, upper, seg_f, seg_r = block_tables(deltas, rates_ref[...], resets_ref, index * length)
    mask_f = (lower > 0.0) & (seg_f[0] == seg_f[1])
    mask_r = (upper > 0.0) & (seg_r[0] == seg_r[1])
    seg_fc, seg_rc = seg_f[0][:, :states], seg_r[0][:, :states]
    end_f, end_r = seg_fc == seg_fc[length - 1 : length], seg_rc == seg_rc[0:1]
    start_f, start_r = seg_fc == 0.0, seg_rc == 0.0
    write, read = write_ref[...], read_ref[...]
    zero = jnp.zeros_like(write)
    write_f, write_r = jnp.where(end_f, write, zero), jnp.where(end_r, write, zero)
    read_f, read_r = jnp.where(start_f, read, zero), jnp.where(start_r, read, zero)
    scores = mm(read, write, NT)
    scores_f = jnp.where(mask_f, scores, 0.0).astype(BF16)
    scores_r = jnp.where(mask_r, scores, 0.0).astype(BF16)
    open_f = jnp.where(seg_f[0][length - 1 : length, 0:1] == 0.0, 1.0, 0.0)
    open_r = jnp.where(seg_r[0][0:1, 0:1] == 0.0, 1.0, 0.0)
    skip = jnp.broadcast_to(skip_ref[...], (8, heads))
    parts = spread_parts(factors(deltas, lam, cum) + [skip])
    flow_f = jnp.zeros((length, heads), F32)
    flow_r = jnp.zeros((length, heads), F32)
    direct = jnp.zeros((length, heads), F32)
    rows = jnp.zeros((8, heads), F32)
    pair_f = jnp.zeros((length, length), F32)
    pair_r = jnp.zeros((length, length), F32)
    acc_read_f = jnp.zeros((length, states), F32)
    acc_read_r = jnp.zeros((length, states), F32)
    acc_write_f = jnp.zeros((length, states), F32)
    acc_write_r = jnp.zeros((length, states), F32)
    for start in range(0, channels, WIDE):
        expand = expander(heads, WIDE, start)
        spread = mm(parts, expand)
        step, u_f, v_f, u_r, v_r = (spread[i * length : (i + 1) * length] for i in range(5))
        gain = spread[5 * length : 5 * length + 1]
        lanes = slice(start, start + WIDE)
        x = x_ref[:, lanes].astype(F32)
        cot = cot_ref[:, lanes].astype(F32)
        scaled = (step * x).astype(BF16).astype(F32)
        chain = u_f[length - 1 : length]
        sc_f, sc_r = (v_f * scaled).astype(BF16), (v_r * scaled).astype(BF16)
        ct_f, ct_r = (u_f * cot).astype(BF16), (u_r * cot).astype(BF16)
        chunk, part, chip = place_of(start, own[0].shape[2], chips)
        entering = []
        for scan in range(4):
            a, b = own[chunk][scan, chip, part], got[chunk][scan, chip, part]
            entering.append(jnp.concatenate([jnp.where(core == 0, a, b), jnp.where(core == 0, b, a)], axis=1))
        in_f, back_r, back_f, in_r = entering
        in_f16, in_r16 = in_f.astype(BF16), (in_r * chain).astype(BF16)
        back_f16, back_r16 = (back_f * chain).astype(BF16), back_r.astype(BF16)
        y_f = u_f * (mm(scores_f, sc_f) + mm(read_f, in_f16))
        y_r = u_r * (mm(scores_r, sc_r) + mm(read_r, in_r16))
        g_f = v_f * (mm(scores_f, ct_f, TN) + mm(write_f, back_f16))
        g_r = v_r * (mm(scores_r, ct_r, TN) + mm(write_r, back_r16))
        out_ref[:, lanes] = (y_f + y_r + gain * x).astype(BF16)
        grad = g_f + g_r
        gin_ref[:, lanes] = (step * grad + gain * cot).astype(BF16)
        local_f, local_r = mm(write_f, sc_f, TN) * chain, mm(write_r, sc_r, TN)
        through = back_f * (local_f + open_f * chain * in_f) + back_r * (local_r + open_r * chain * in_r)
        through = jnp.sum(through, axis=0, keepdims=True)
        own_skip = jnp.sum(x * cot, axis=0, keepdims=True)
        small = jnp.concatenate([through, own_skip, jnp.zeros((6, WIDE), F32)], axis=0)
        flows = jnp.concatenate([cot * y_f - scaled * g_f, cot * y_r - scaled * g_r, x * grad, small], axis=0)
        high, low = halves(flows)
        collect = expand[:heads]
        sums = mm(high, collect, NT) + mm(low, collect, NT)
        flow_f = flow_f + sums[:length]
        flow_r = flow_r + sums[length : 2 * length]
        direct = direct + sums[2 * length : 3 * length]
        rows = rows + sums[3 * length :]
        pair_f = pair_f + mm(ct_f, sc_f, NT)
        pair_r = pair_r + mm(ct_r, sc_r, NT)
        acc_read_f = acc_read_f + mm(ct_f, in_f16, NT)
        acc_read_r = acc_read_r + mm(ct_r, in_r16, NT)
        acc_write_f = acc_write_f + mm(sc_f, back_f16, NT)
        acc_write_r = acc_write_r + mm(sc_r, back_r16, NT)
    pairs = (jnp.where(mask_f, pair_f, 0.0) + jnp.where(mask_r, pair_r, 0.0)).astype(BF16)
    gread_ref[...] = mm(pairs, write) + jnp.where(start_f, acc_read_f, 0.0) + jnp.where(start_r, acc_read_r, 0.0)
    gwrite_ref[...] = mm(pairs, read, TN) + jnp.where(end_f, acc_write_f, 0.0) + jnp.where(end_r, acc_write_r, 0.0)
    logs = exact(upper, flow_f) + exact(lower, flow_r) + rows[0:1]
    steps_ref[...] = direct - rates * logs
    small_ref[0:1] = -rates * jnp.sum(deltas * logs, axis=0, keepdims=True)
    small_ref[1:2] = rows[1:2]


def call(body, out_shape, scalars, count, flops, size, name):
    in_specs = [pl.BlockSpec(memory_space=pltpu.SMEM if i in scalars else pltpu.VMEM) for i in range(count)]
    return pl.pallas_call(
        body,
        out_shape=out_shape,
        in_specs=in_specs,
        out_specs=jax.tree.map(lambda _: pl.BlockSpec(memory_space=pltpu.VMEM), out_shape),
        compiler_params=pltpu.CompilerParams(vmem_limit_bytes=40 << 20),
        cost_estimate=pl.CostEstimate(flops=flops, bytes_accessed=size, transcendentals=0),
        name=name,
    )


def local(chips, inputs, step_sizes, write_vecs, read_vecs, log_rates, skip_gain, resets, cotangent):
    x, deltas, write, read, cot = inputs[0], step_sizes[0], write_vecs[0], read_vecs[0], cotangent[0]
    length, channels = x.shape
    heads, states = deltas.shape[1], write.shape[1]
    devices = lax.axis_size("seq")
    planes = devices // (2 * chips)
    levels = int(math.log2(planes))
    chunks = min(CHUNKS, channels // (WIDE * chips))
    parts = channels // (WIDE * chips * chunks)
    rates, skip = log_rates[None], skip_gain[None]

    def like(*shape, kind=F32):
        return jax.ShapeDtypeStruct(shape, kind)

    table = call(totals_kernel, like(1, 2 * heads), (2,), 3, 10000, 20000, "totals")(deltas, rates, resets)
    reach = 1
    while reach < devices:
        far = lax.ppermute(table, "seq", [(i, i ^ reach) for i in range(devices)])
        table = jnp.concatenate([table, far], axis=0)
        reach *= 2

    group = like(4, chips, parts, states, LANES)
    single = like(4, parts, states, LANES)
    half = like(2, parts, states, LANES)
    made = call(functools.partial(states_kernel, chunks, chips), [group] * (2 * chunks), (6,), 7, 300 * 10**6, 4 * 10**6, "states")(
        x, cot, deltas, write, read, rates, resets
    )
    keep, send = made[:chunks], made[chunks:]

    def device(plane, chip, core):
        return (plane * chips + chip) * 2 + core

    every = [(p, a, c) for p in range(planes) for a in range(chips) for c in range(2)]
    swap = [(device(p, a, c), device(p, a, 1 - c)) for p, a, c in every]

    def turn(shift):
        return [(device(p, a, c), device(p, (a + shift) % chips, c)) for p, a, c in every]

    def across(level):
        return [(device(p, a, c), device(p ^ 2**level, a, c)) for p, a, c in every]

    def send_to(value, perm):
        return lax.ppermute(value, "seq", perm)

    size = 4 * parts * states * LANES * 4
    owns, gots = [], []
    for k in range(chunks):
        got = send_to(send[k], swap)
        chip_totals = call(functools.partial(chip_kernel, k, chips, heads), [single] * chips, (0,), 3, 10**6, size * 6, "chip")(
            table, keep[k], got
        )
        gathered = [chip_totals[0]] + [None] * (chips - 1)
        for shift in range(1, chips):
            gathered[chips - shift] = send_to(chip_totals[shift], turn(shift))
        (onward,) = call(functools.partial(plane_kernel, k, chips, heads), [single], (0,), 1 + chips, 10**6, size * 3, "plane")(table, *gathered)
        before = []
        for level in range(levels - 1):
            arrived = send_to(onward, across(level))
            last = level == levels - 2
            hop = call(
                functools.partial(hop_kernel, k, chips, heads, level, last),
                [single, half if last else single],
                (0,),
                3 + len(before),
                10**6,
                size * 4,
                "hop",
            )
            entry, onward = hop(table, *before, onward, arrived)
            before = [entry]
        arrived = send_to(onward, across(levels - 1))
        placed = call(
            functools.partial(spread_kernel, k, chips, heads, levels - 1), [single] * chips, (0,), 3 + chips, 10**6, size * 5, "spread"
        )(table, *before, arrived, *gathered)
        entered = [placed[0]] + [send_to(placed[shift], turn(shift)) for shift in range(1, chips)]
        mine, theirs = call(functools.partial(core_kernel, k, chips, heads), [group] * 2, (0,), 3 + chips, 10**6, size * 8, "core")(
            table, keep[k], got, *entered
        )
        owns.append(mine)
        gots.append(send_to(theirs, swap))

    outputs, grad_inputs, grad_steps, grad_write, grad_read, small = call(
        functools.partial(finish_kernel, chunks, chips),
        [
            like(length, channels, kind=BF16),
            like(length, channels, kind=BF16),
            like(length, heads),
            like(length, states),
            like(length, states),
            like(2, heads),
        ],
        (7,),
        8 + 2 * chunks,
        2 * 10**9,
        6 * 10**6,
        "finish",
    )(x, cot, deltas, write, read, rates, skip, resets, *owns, *gots)
    count = devices * lax.axis_size("dp")
    spread = jnp.broadcast_to(small[None], (count,) + small.shape)
    total = jnp.sum(lax.all_to_all(spread, ("seq", "dp"), 0, 0, tiled=True), axis=0)
    return (outputs[None], grad_inputs[None], grad_steps[None], grad_write[None], grad_read[None], total[0], total[1])


def solution(mesh):
    along = P("dp", "seq", None)
    chips = 2 ** (int(math.log2(mesh.shape["seq"] // 2)) // 2)
    return jax.shard_map(
        functools.partial(local, chips),
        mesh=mesh,
        in_specs=(along, along, along, along, P(), P(), P("dp", None), along),
        out_specs=(along, along, along, along, along, P(), P()),
        check_vma=False,
    )
```

time: 440 us -> 84.4 us (0.19); the launches traced: 433 us -> 84 us
  local copies, waits for them, and re-layouts: 132 us -> 7.81 us
  other arithmetic: 90.6 us -> 0.07 us
  blocking collectives: 79.9 us -> 0 us
  matrix products: 74.5 us -> 0 us
  starting transfers between devices: 0.16 us -> 36.3 us
  Pallas kernels: 0 us -> 26.2 us
  waiting for transfers between devices: 38.5 us -> 12.7 us
  between operations: 15.6 us -> 0.93 us
    dot_general x42 -> x0, matrix products: 74.5 us -> none  [the longest x8 15.9 us: block_local(): jnp.einsum('gts,tgp->sgp', weights, grad_part, preferred_element_type=jnp...]
    select_n x60 -> x0, other arithmetic: 70.2 us -> none  [hop(): jnp.where(position < mine, new, old)]
    mul x64 -> x0, local copies, waits for them, and re-layouts: 42.4 us -> none  [the longest x60 41.3 us: combine_link(): return (earlier[0] * later[0], later[1] + later[0][:, None] * earlier[1])]
    all_gather x2 -> x0, blocking collectives: 41 us -> none  [prefix(): pieces = jax.tree.map(lambda part: lax.all_gather(part, axis), value)]
    psum x1 -> x0, blocking collectives: 38.9 us -> none  [local(): grad_rates, grad_skip = lax.psum((rate_part, skip_part), ('seq', 'dp'))]
    all_gather x4 -> x0, waiting for transfers between devices: 38.4 us -> none  [prefix(): pieces = jax.tree.map(lambda part: lax.all_gather(part, axis), value)]
    ppermute x0 -> x28, starting transfers between devices: none -> 31.5 us  [the longest x24 22.8 us: send_to(): return lax.ppermute(value, 'seq', perm)]
    rev x27 -> x0, local copies, waits for them, and re-layouts: 27.5 us -> none  [the longest x4 16.4 us: prefix(): pieces = jax.tree.map(lambda part: part[::-1], pieces)]
  transfers between devices with their start and end apart: 4 -> 29, of which waited for: 2 -> 6; matrix products, arithmetic and copies ran while one was open for 54% -> 3% of each run, Pallas kernels for 0% -> 23%
where the time goes in v1:
time: 84.4 us; the launch traced here: 84 us
  starting transfers between devices  36.3 us (43%)
  Pallas kernels  26.2 us (31%)
  waiting for transfers between devices  12.7 us (15%)
  local copies, waits for them, and re-layouts  7.81 us (9%)
  between operations  0.93 us (1%)
    ppermute x24, starting transfers between devices, send_to(): return lax.ppermute(value, 'seq', perm)  22.8 us
    ppermute x4, starting transfers between devices, local(): far = lax.ppermute(table, 'seq', [(i, i ^ reach) for i in range(devices)])  8.72 us
    unnamed x24, local copies, waits for them, and re-layouts  6.65 us
    pallas_call x1, Pallas kernels, local(): call(functools.partial(finish_kernel, chunks, chips), [like(length, chann...  6.5 us
    all_to_all x1, waiting for transfers between devices, local(): lax.all_to_all(spread, ('seq', 'dp'), 0, 0, tiled=True)  5.27 us
    all_to_all x1, starting transfers between devices, local(): lax.all_to_all(spread, ('seq', 'dp'), 0, 0, tiled=True)  4.82 us
    ppermute x4, waiting for transfers between devices, local(): far = lax.ppermute(table, 'seq', [(i, i ^ reach) for i in range(devices)])  4.7 us
    pallas_call x1, Pallas kernels, local(): call(functools.partial(states_kernel, chunks, chips), [group] * (2 * chun...  3.6 us
  transfers between devices with their start and end apart: 29, of which 6 were waited for; matrix products, arithmetic and copies ran while one was open for 3% of the time, Pallas kernels for 23%

profile of v1, /device:TPU:0, one launch (start us, length us, event | category | flops | bytes accessed | tf_op | source)
XLA Modules:
  0.0 84.0 jit_solution(10123351433054557257)
XLA Ops:
  3.6 1.0 %copy-done = bf16[1,128,2048]{2,1,0:T(8,128)(2,1)S(1)} copy-done((bf16[1,128,2048]{2,1,0:T(8,128)(2,1)S(1)}, bf16[1,128,2048]{2,1,0:T(8,128)(2,1)}, u32[]{:S(2)}) %copy-start) | copy-done | bytes 524312
  4.7 1.0 %copy-done.2 = bf16[1,128,2048]{2,1,0:T(8,128)(2,1)S(1)} copy-done((bf16[1,128,2048]{2,1,0:T(8,128)(2,1)S(1)}, bf16[1,128,2048]{2,1,0:T(8,128)(2,1)}, u32[]{:S(2)}) %copy-start.2) | copy-done | bytes 524312
  5.7 3.6 %states.1 = (f32[4,2,1,64,128]{4,3,2,1,0:T(8,128)S(1)}, f32[4,2,1,64,128]{4,3,2,1,0:T(8,128)S(1)}, f32[4,2,1,64,128]{4,3,2,1,0:T(8,128)S(1)}, f32[4,2,1,64,128]{...) custom-call(bf16[128,2048]{1,0:T(8,128)(2,1)S(1)} %bitcast.19, ...), custom_call_target="tpu_custom_call" | custom-call | flops 300000000 | bytes 4000000 | tf_op jit(solution)/shard_map/states/pallas_call | solution.py:449
  10.4 3.0 %collective-permute-start.1 = (f32[2,64]{1,0:T(2,128)S(1)}, f32[2,64]{1,0:T(2,128)S(1)}, u32[]{:S(2)}, u32[]{:S(2)}) collective-permute-start(f32[2,64]{1,0:T(2,128)S(1)} %pad_maximum_fusion.2), channel_id=1, source_target_pairs={{0,4},{2,6},{4,0},{6,2},{8,12},{10,14},{12,8},{14,10},{16,20},{18,... | collective-permute-start | bytes 1544 | tf_op jit(solution)/shard_map/ppermute | solution.py:442
  13.4 1.5 %collective-permute-done.1 = f32[2,64]{1,0:T(2,128)S(1)} collective-permute-done((f32[2,64]{1,0:T(2,128)S(1)}, f32[2,64]{1,0:T(2,128)S(1)}, u32[]{:S(2)}, u32[]{:S(2)}) %collective-permute-start.1) | collective-permute-done | bytes 544 | tf_op jit(solution)/shard_map/ppermute | solution.py:442
  15.0 2.2 %collective-permute-start.2 = (f32[4,64]{1,0:T(4,128)S(1)}, f32[4,64]{1,0:T(4,128)S(1)}, u32[]{:S(2)}, u32[]{:S(2)}) collective-permute-start(f32[4,64]{1,0:T(4,128)S(1)} %pad_maximum_fusion.1), channel_id=1, source_target_pairs={{0,8},{2,10},{4,12},{6,14},{8,0},{10,2},{12,4},{14,6},{16,24},{18,... | collective-permute-start | bytes 3080 | tf_op jit(solution)/shard_map/ppermute | solution.py:442
  17.1 1.6 %collective-permute-done.2 = f32[4,64]{1,0:T(4,128)S(1)} collective-permute-done((f32[4,64]{1,0:T(4,128)S(1)}, f32[4,64]{1,0:T(4,128)S(1)}, u32[]{:S(2)}, u32[]{:S(2)}) %collective-permute-start.2) | collective-permute-done | bytes 1056 | tf_op jit(solution)/shard_map/ppermute | solution.py:442
  18.7 3.1 %collective-permute-start.3 = (f32[8,64]{1,0:T(8,128)S(1)}, f32[8,64]{1,0:T(8,128)S(1)}, u32[]{:S(2)}, u32[]{:S(2)}) collective-permute-start(f32[8,64]{1,0:T(8,128)S(1)} %pad_maximum_fusion), channel_id=1, source_target_pairs={{0,16},{2,18},{4,20},{6,22},{8,24},{10,26},{12,28},{14,30},{16,0},... | collective-permute-start | bytes 6152 | tf_op jit(solution)/shard_map/ppermute | solution.py:442
  21.8 1.6 %collective-permute-done.3 = f32[8,64]{1,0:T(8,128)S(1)} collective-permute-done((f32[8,64]{1,0:T(8,128)S(1)}, f32[8,64]{1,0:T(8,128)S(1)}, u32[]{:S(2)}, u32[]{:S(2)}) %collective-permute-start.3) | collective-permute-done | bytes 2080 | tf_op jit(solution)/shard_map/ppermute | solution.py:442
  24.2 1.9 %collective-permute-start.5 = (f32[4,1,64,128]{3,2,1,0:T(8,128)S(1)}, f32[4,1,64,128]{3,2,1,0:T(8,128)S(1)}, u32[]{:S(2)}, u32[]{:S(2)}) collective-permute-start(f32[4,1,64,128]{3,2,1,0:T(8,128)S(1)} %get-tuple-element.56), channel_id=1, source_target_pairs={{0,4},{2,6},{4,0},{6,2},{8,12},{10,14},{12,8},{14,10},{16,20},{18,... | collective-permute-start | bytes 393224 | tf_op jit(solution)/shard_map/ppermute | solution.py:467
  27.8 1.9 %collective-permute-start.15 = (f32[4,1,64,128]{3,2,1,0:T(8,128)S(1)}, f32[4,1,64,128]{3,2,1,0:T(8,128)S(1)}, u32[]{:S(2)}, u32[]{:S(2)}) collective-permute-start(f32[4,1,64,128]{3,2,1,0:T(8,128)S(1)} %get-tuple-element.74), channel_id=1, source_target_pairs={{0,4},{2,6},{4,0},{6,2},{8,12},{10,14},{12,8},{14,10},{16,20},{18,... | collective-permute-start | bytes 393224 | tf_op jit(solution)/shard_map/ppermute | solution.py:467
  31.5 2.0 %collective-permute-start.6 = (f32[4,1,64,128]{3,2,1,0:T(8,128)S(1)}, f32[4,1,64,128]{3,2,1,0:T(8,128)S(1)}, u32[]{:S(2)}, u32[]{:S(2)}) collective-permute-start(f32[4,1,64,128]{3,2,1,0:T(8,128)S(1)} %plane.4.refs_0_), channel_id=1, source_target_pairs={{0,8},{2,10},{4,12},{6,14},{8,0},{10,2},{12,4},{14,6},{16,24},{18,... | collective-permute-start | bytes 393224 | tf_op jit(solution)/shard_map/ppermute | solution.py:467
  36.0 1.1 %collective-permute-start.16 = (f32[4,1,64,128]{3,2,1,0:T(8,128)S(1)}, f32[4,1,64,128]{3,2,1,0:T(8,128)S(1)}, u32[]{:S(2)}, u32[]{:S(2)}) collective-permute-start(f32[4,1,64,128]{3,2,1,0:T(8,128)S(1)} %plane.6.refs_0_), channel_id=1, source_target_pairs={{0,8},{2,10},{4,12},{6,14},{8,0},{10,2},{12,4},{14,6},{16,24},{18,... | collective-permute-start | bytes 393224 | tf_op jit(solution)/shard_map/ppermute | solution.py:467
  39.7 2.7 %collective-permute-start.7 = (f32[2,1,64,128]{3,2,1,0:T(8,128)S(1)}, f32[2,1,64,128]{3,2,1,0:T(8,128)S(1)}, u32[]{:S(2)}, u32[]{:S(2)}) collective-permute-start(f32[2,1,64,128]{3,2,1,0:T(8,128)S(1)} %get-tuple-element.58), channel_id=1, source_target_pairs={{0,16},{2,18},{4,20},{6,22},{8,24},{10,26},{12,28},{14,30},{16,0},... | collective-permute-start | bytes 196616 | tf_op jit(solution)/shard_map/ppermute | solution.py:467
  43.1 1.4 %collective-permute-start.12 = (f32[2,1,64,128]{3,2,1,0:T(8,128)S(1)}, f32[2,1,64,128]{3,2,1,0:T(8,128)S(1)}, u32[]{:S(2)}, u32[]{:S(2)}) collective-permute-start(f32[2,1,64,128]{3,2,1,0:T(8,128)S(1)} %get-tuple-element.67), channel_id=1, source_target_pairs={{0,16},{2,18},{4,20},{6,22},{8,24},{10,26},{12,28},{14,30},{16,0},... | collective-permute-start | bytes 196616 | tf_op jit(solution)/shard_map/ppermute | solution.py:467
  45.3 1.7 %collective-permute-start.17 = (f32[2,1,64,128]{3,2,1,0:T(8,128)S(1)}, f32[2,1,64,128]{3,2,1,0:T(8,128)S(1)}, u32[]{:S(2)}, u32[]{:S(2)}) collective-permute-start(f32[2,1,64,128]{3,2,1,0:T(8,128)S(1)} %get-tuple-element.76), channel_id=1, source_target_pairs={{0,16},{2,18},{4,20},{6,22},{8,24},{10,26},{12,28},{14,30},{16,0},... | collective-permute-start | bytes 196616 | tf_op jit(solution)/shard_map/ppermute | solution.py:467
  47.8 1.4 %collective-permute-start.22 = (f32[2,1,64,128]{3,2,1,0:T(8,128)S(1)}, f32[2,1,64,128]{3,2,1,0:T(8,128)S(1)}, u32[]{:S(2)}, u32[]{:S(2)}) collective-permute-start(f32[2,1,64,128]{3,2,1,0:T(8,128)S(1)} %get-tuple-element.85), channel_id=1, source_target_pairs={{0,16},{2,18},{4,20},{6,22},{8,24},{10,26},{12,28},{14,30},{16,0},... | collective-permute-start | bytes 196616 | tf_op jit(solution)/shard_map/ppermute | solution.py:467
  50.0 1.4 %collective-permute-start.8 = (f32[4,1,64,128]{3,2,1,0:T(8,128)S(1)}, f32[4,1,64,128]{3,2,1,0:T(8,128)S(1)}, u32[]{:S(2)}, u32[]{:S(2)}) collective-permute-start(f32[4,1,64,128]{3,2,1,0:T(8,128)S(1)} %get-tuple-element.60), channel_id=1, source_target_pairs={{0,4},{2,6},{4,0},{6,2},{8,12},{10,14},{12,8},{14,10},{16,20},{18,... | collective-permute-start | bytes 393224 | tf_op jit(solution)/shard_map/ppermute | solution.py:467
  53.9 1.4 %collective-permute-start.18 = (f32[4,1,64,128]{3,2,1,0:T(8,128)S(1)}, f32[4,1,64,128]{3,2,1,0:T(8,128)S(1)}, u32[]{:S(2)}, u32[]{:S(2)}) collective-permute-start(f32[4,1,64,128]{3,2,1,0:T(8,128)S(1)} %get-tuple-element.78), channel_id=1, source_target_pairs={{0,4},{2,6},{4,0},{6,2},{8,12},{10,14},{12,8},{14,10},{16,20},{18,... | collective-permute-start | bytes 393224 | tf_op jit(solution)/shard_map/ppermute | solution.py:467
  60.0 1.2 %collective-permute-done.23.refs_1_ = f32[4,1,64,128]{3,2,1,0:T(8,128)S(1)} collective-permute-done((f32[4,1,64,128]{3,2,1,0:T(8,128)S(1)}, f32[4,1,64,128]{3,2,1,0:T(8,128)S(1)}, u32[]{:S(2)}, u32[]{:S(2)}) %collective-permute-start.23) | collective-permute-done | bytes 131104 | tf_op jit(solution)/shard_map/ppermute | solution.py:467
  62.0 1.5 %collective-permute-done.27.refs_7_ = f32[4,2,1,64,128]{4,3,2,1,0:T(8,128)S(1)} collective-permute-done((f32[4,2,1,64,128]{4,3,2,1,0:T(8,128)S(1)}, f32[4,2,1,64,128]{4,3,2,1,0:T(8,128)S(1)}, u32[]{:S(2)}, u32[]{:S(2)}) %collective-permute-start.27) | collective-permute-done | bytes 262176 | tf_op jit(solution)/shard_map/ppermute | solution.py:467
  64.2 6.5 %finish.1 = (bf16[128,2048]{1,0:T(8,128)(2,1)}, bf16[128,2048]{1,0:T(8,128)(2,1)}, f32[128,32]{1,0:T(8,128)S(1)}, f32[128,64]{1,0:T(8,128)S(1)}, f32[128,64]{1,0:T(8,128)S(1)}, /*index=5*/f32[2,32]{1,0:T(2,128)S(1)}) custom-call(bf16[128,2048]{1,0:T(8,128)(2,1)S(1)} %bitcast.20, bf16[128,2048]{1,0:T(8,128)(2,1)S(1)} %bitcast.22, f32[128,32]{1,0:T(8,128)S(1)} %bitcast.18, ...), custom_call_target="tpu_custom_call" | custom-call | flops 2000000000 | bytes 6000000 | tf_op jit(solution)/shard_map/finish/pallas_call | solution.py:506
  71.3 4.8 %all-to-all-start = ((f32[32,2,32]{2,1,0:T(2,128)}), f32[32,2,32]{2,1,0:T(2,128)S(1)}, u32[]{:S(2)}, u32[]{:S(2)}) async-start(f32[32,2,32]{2,1,0:T(2,128)} %broadcast_in_dim.34), calls=%async_computation | async-start | bytes 65536 | tf_op jit(solution)/shard_map/all_to_all | solution.py:524
  78.2 5.3 %all-to-all-done = f32[32,2,32]{2,1,0:T(2,128)S(1)} async-done(((f32[32,2,32]{2,1,0:T(2,128)}), f32[32,2,32]{2,1,0:T(2,128)S(1)}, u32[]{:S(2)}, u32[]{:S(2)}) %all-to-all-start) | async-done | bytes 8224 | tf_op jit(solution)/shard_map/all_to_all | solution.py:524
  (88 shorter events, 28.6 us)
Async XLA Ops:
  2.8 7.7 %collective-permute-start = (f32[1,64]{1,0:T(1,128)S(1)}, f32[1,64]{1,0:T(1,128)S(1)}, u32[]{:S(2)}, u32[]{:S(2)}) collective-permute-start(f32[1,64]{1,0:T(1,128)S(1)} %totals.1), channel_id=1, source_target_pairs={{0,2},{2,0},{4,6},{6,4},{8,10},{10,8},{12,14},{14,12},{16,18},{18,... | collective-permute-start | bytes 776 | tf_op jit(solution)/shard_map/ppermute | solution.py:442
  9.3 14.1 %collective-permute-start.4 = (f32[4,2,1,64,128]{4,3,2,1,0:T(8,128)S(1)}, f32[4,2,1,64,128]{4,3,2,1,0:T(8,128)S(1)}, u32[]{:S(2)}, u32[]{:S(2)}) collective-permute-start(f32[4,2,1,64,128]{4,3,2,1,0:T(8,128)S(1)} %get-tuple-element.54), channel_id=1, source_target_pairs={{0,2},{2,0},{4,6},{6,4},{8,10},{10,8},{12,14},{14,12},{16,18},{18,... | collective-permute-start | bytes 786440 | tf_op jit(solution)/shard_map/ppermute | solution.py:467
  9.8 16.2 %collective-permute-start.9 = (f32[4,2,1,64,128]{4,3,2,1,0:T(8,128)S(1)}, f32[4,2,1,64,128]{4,3,2,1,0:T(8,128)S(1)}, u32[]{:S(2)}, u32[]{:S(2)}) collective-permute-start(f32[4,2,1,64,128]{4,3,2,1,0:T(8,128)S(1)} %get-tuple-element.63), channel_id=1, source_target_pairs={{0,2},{2,0},{4,6},{6,4},{8,10},{10,8},{12,14},{14,12},{16,18},{18,... | collective-permute-start | bytes 786440 | tf_op jit(solution)/shard_map/ppermute | solution.py:467
  9.9 17.2 %collective-permute-start.14 = (f32[4,2,1,64,128]{4,3,2,1,0:T(8,128)S(1)}, f32[4,2,1,64,128]{4,3,2,1,0:T(8,128)S(1)}, u32[]{:S(2)}, u32[]{:S(2)}) collective-permute-start(f32[4,2,1,64,128]{4,3,2,1,0:T(8,128)S(1)} %get-tuple-element.72), channel_id=1, source_target_pairs={{0,2},{2,0},{4,6},{6,4},{8,10},{10,8},{12,14},{14,12},{16,18},{18,... | collective-permute-start | bytes 786440 | tf_op jit(solution)/shard_map/ppermute | solution.py:467
  10.3 19.4 %collective-permute-start.19 = (f32[4,2,1,64,128]{4,3,2,1,0:T(8,128)S(1)}, f32[4,2,1,64,128]{4,3,2,1,0:T(8,128)S(1)}, u32[]{:S(2)}, u32[]{:S(2)}) collective-permute-start(f32[4,2,1,64,128]{4,3,2,1,0:T(8,128)S(1)} %get-tuple-element.81), channel_id=1, source_target_pairs={{0,2},{2,0},{4,6},{6,4},{8,10},{10,8},{12,14},{14,12},{16,18},{18,... | collective-permute-start | bytes 786440 | tf_op jit(solution)/shard_map/ppermute | solution.py:467
  10.4 4.5 %collective-permute-start.1 = (f32[2,64]{1,0:T(2,128)S(1)}, f32[2,64]{1,0:T(2,128)S(1)}, u32[]{:S(2)}, u32[]{:S(2)}) collective-permute-start(f32[2,64]{1,0:T(2,128)S(1)} %pad_maximum_fusion.2), channel_id=1, source_target_pairs={{0,4},{2,6},{4,0},{6,2},{8,12},{10,14},{12,8},{14,10},{16,20},{18,... | collective-permute-start | bytes 1544 | tf_op jit(solution)/shard_map/ppermute | solution.py:442
  18.7 4.7 %collective-permute-start.3 = (f32[8,64]{1,0:T(8,128)S(1)}, f32[8,64]{1,0:T(8,128)S(1)}, u32[]{:S(2)}, u32[]{:S(2)}) collective-permute-start(f32[8,64]{1,0:T(8,128)S(1)} %pad_maximum_fusion), channel_id=1, source_target_pairs={{0,16},{2,18},{4,20},{6,22},{8,24},{10,26},{12,28},{14,30},{16,0},... | collective-permute-start | bytes 6152 | tf_op jit(solution)/shard_map/ppermute | solution.py:442
  24.2 6.6 %collective-permute-start.5 = (f32[4,1,64,128]{3,2,1,0:T(8,128)S(1)}, f32[4,1,64,128]{3,2,1,0:T(8,128)S(1)}, u32[]{:S(2)}, u32[]{:S(2)}) collective-permute-start(f32[4,1,64,128]{3,2,1,0:T(8,128)S(1)} %get-tuple-element.56), channel_id=1, source_target_pairs={{0,4},{2,6},{4,0},{6,2},{8,12},{10,14},{12,8},{14,10},{16,20},{18,... | collective-permute-start | bytes 393224 | tf_op jit(solution)/shard_map/ppermute | solution.py:467
  26.8 6.6 %collective-permute-start.10 = (f32[4,1,64,128]{3,2,1,0:T(8,128)S(1)}, f32[4,1,64,128]{3,2,1,0:T(8,128)S(1)}, u32[]{:S(2)}, u32[]{:S(2)}) collective-permute-start(f32[4,1,64,128]{3,2,1,0:T(8,128)S(1)} %get-tuple-element.65), channel_id=1, source_target_pairs={{0,4},{2,6},{4,0},{6,2},{8,12},{10,14},{12,8},{14,10},{16,20},{18,... | collective-permute-start | bytes 393224 | tf_op jit(solution)/shard_map/ppermute | solution.py:467
  27.8 7.4 %collective-permute-start.15 = (f32[4,1,64,128]{3,2,1,0:T(8,128)S(1)}, f32[4,1,64,128]{3,2,1,0:T(8,128)S(1)}, u32[]{:S(2)}, u32[]{:S(2)}) collective-permute-start(f32[4,1,64,128]{3,2,1,0:T(8,128)S(1)} %get-tuple-element.74), channel_id=1, source_target_pairs={{0,4},{2,6},{4,0},{6,2},{8,12},{10,14},{12,8},{14,10},{16,20},{18,... | collective-permute-start | bytes 393224 | tf_op jit(solution)/shard_map/ppermute | solution.py:467
  30.5 6.7 %collective-permute-start.20 = (f32[4,1,64,128]{3,2,1,0:T(8,128)S(1)}, f32[4,1,64,128]{3,2,1,0:T(8,128)S(1)}, u32[]{:S(2)}, u32[]{:S(2)}) collective-permute-start(f32[4,1,64,128]{3,2,1,0:T(8,128)S(1)} %get-tuple-element.83), channel_id=1, source_target_pairs={{0,4},{2,6},{4,0},{6,2},{8,12},{10,14},{12,8},{14,10},{16,20},{18,... | collective-permute-start | bytes 393224 | tf_op jit(solution)/shard_map/ppermute | solution.py:467
  31.5 7.4 %collective-permute-start.6 = (f32[4,1,64,128]{3,2,1,0:T(8,128)S(1)}, f32[4,1,64,128]{3,2,1,0:T(8,128)S(1)}, u32[]{:S(2)}, u32[]{:S(2)}) collective-permute-start(f32[4,1,64,128]{3,2,1,0:T(8,128)S(1)} %plane.4.refs_0_), channel_id=1, source_target_pairs={{0,8},{2,10},{4,12},{6,14},{8,0},{10,2},{12,4},{14,6},{16,24},{18,... | collective-permute-start | bytes 393224 | tf_op jit(solution)/shard_map/ppermute | solution.py:467
  34.2 8.1 %collective-permute-start.11 = (f32[4,1,64,128]{3,2,1,0:T(8,128)S(1)}, f32[4,1,64,128]{3,2,1,0:T(8,128)S(1)}, u32[]{:S(2)}, u32[]{:S(2)}) collective-permute-start(f32[4,1,64,128]{3,2,1,0:T(8,128)S(1)} %plane.5.refs_0_), channel_id=1, source_target_pairs={{0,8},{2,10},{4,12},{6,14},{8,0},{10,2},{12,4},{14,6},{16,24},{18,... | collective-permute-start | bytes 393224 | tf_op jit(solution)/shard_map/ppermute | solution.py:467
  36.0 8.5 %collective-permute-start.16 = (f32[4,1,64,128]{3,2,1,0:T(8,128)S(1)}, f32[4,1,64,128]{3,2,1,0:T(8,128)S(1)}, u32[]{:S(2)}, u32[]{:S(2)}) collective-permute-start(f32[4,1,64,128]{3,2,1,0:T(8,128)S(1)} %plane.6.refs_0_), channel_id=1, source_target_pairs={{0,8},{2,10},{4,12},{6,14},{8,0},{10,2},{12,4},{14,6},{16,24},{18,... | collective-permute-start | bytes 393224 | tf_op jit(solution)/shard_map/ppermute | solution.py:467
  37.9 9.1 %collective-permute-start.21 = (f32[4,1,64,128]{3,2,1,0:T(8,128)S(1)}, f32[4,1,64,128]{3,2,1,0:T(8,128)S(1)}, u32[]{:S(2)}, u32[]{:S(2)}) collective-permute-start(f32[4,1,64,128]{3,2,1,0:T(8,128)S(1)} %plane.7.refs_0_), channel_id=1, source_target_pairs={{0,8},{2,10},{4,12},{6,14},{8,0},{10,2},{12,4},{14,6},{16,24},{18,... | collective-permute-start | bytes 393224 | tf_op jit(solution)/shard_map/ppermute | solution.py:467
  39.7 9.5 %collective-permute-start.7 = (f32[2,1,64,128]{3,2,1,0:T(8,128)S(1)}, f32[2,1,64,128]{3,2,1,0:T(8,128)S(1)}, u32[]{:S(2)}, u32[]{:S(2)}) collective-permute-start(f32[2,1,64,128]{3,2,1,0:T(8,128)S(1)} %get-tuple-element.58), channel_id=1, source_target_pairs={{0,16},{2,18},{4,20},{6,22},{8,24},{10,26},{12,28},{14,30},{16,0},... | collective-permute-start | bytes 196616 | tf_op jit(solution)/shard_map/ppermute | solution.py:467
  43.1 8.2 %collective-permute-start.12 = (f32[2,1,64,128]{3,2,1,0:T(8,128)S(1)}, f32[2,1,64,128]{3,2,1,0:T(8,128)S(1)}, u32[]{:S(2)}, u32[]{:S(2)}) collective-permute-start(f32[2,1,64,128]{3,2,1,0:T(8,128)S(1)} %get-tuple-element.67), channel_id=1, source_target_pairs={{0,16},{2,18},{4,20},{6,22},{8,24},{10,26},{12,28},{14,30},{16,0},... | collective-permute-start | bytes 196616 | tf_op jit(solution)/shard_map/ppermute | solution.py:467
  45.3 7.7 %collective-permute-start.17 = (f32[2,1,64,128]{3,2,1,0:T(8,128)S(1)}, f32[2,1,64,128]{3,2,1,0:T(8,128)S(1)}, u32[]{:S(2)}, u32[]{:S(2)}) collective-permute-start(f32[2,1,64,128]{3,2,1,0:T(8,128)S(1)} %get-tuple-element.76), channel_id=1, source_target_pairs={{0,16},{2,18},{4,20},{6,22},{8,24},{10,26},{12,28},{14,30},{16,0},... | collective-permute-start | bytes 196616 | tf_op jit(solution)/shard_map/ppermute | solution.py:467
  47.8 7.5 %collective-permute-start.22 = (f32[2,1,64,128]{3,2,1,0:T(8,128)S(1)}, f32[2,1,64,128]{3,2,1,0:T(8,128)S(1)}, u32[]{:S(2)}, u32[]{:S(2)}) collective-permute-start(f32[2,1,64,128]{3,2,1,0:T(8,128)S(1)} %get-tuple-element.85), channel_id=1, source_target_pairs={{0,16},{2,18},{4,20},{6,22},{8,24},{10,26},{12,28},{14,30},{16,0},... | collective-permute-start | bytes 196616 | tf_op jit(solution)/shard_map/ppermute | solution.py:467
  50.0 6.9 %collective-permute-start.8 = (f32[4,1,64,128]{3,2,1,0:T(8,128)S(1)}, f32[4,1,64,128]{3,2,1,0:T(8,128)S(1)}, u32[]{:S(2)}, u32[]{:S(2)}) collective-permute-start(f32[4,1,64,128]{3,2,1,0:T(8,128)S(1)} %get-tuple-element.60), channel_id=1, source_target_pairs={{0,4},{2,6},{4,0},{6,2},{8,12},{10,14},{12,8},{14,10},{16,20},{18,... | collective-permute-start | bytes 393224 | tf_op jit(solution)/shard_map/ppermute | solution.py:467
  52.2 5.5 %collective-permute-start.13 = (f32[4,1,64,128]{3,2,1,0:T(8,128)S(1)}, f32[4,1,64,128]{3,2,1,0:T(8,128)S(1)}, u32[]{:S(2)}, u32[]{:S(2)}) collective-permute-start(f32[4,1,64,128]{3,2,1,0:T(8,128)S(1)} %get-tuple-element.69), channel_id=1, source_target_pairs={{0,4},{2,6},{4,0},{6,2},{8,12},{10,14},{12,8},{14,10},{16,20},{18,... | collective-permute-start | bytes 393224 | tf_op jit(solution)/shard_map/ppermute | solution.py:467
  53.9 5.2 %collective-permute-start.18 = (f32[4,1,64,128]{3,2,1,0:T(8,128)S(1)}, f32[4,1,64,128]{3,2,1,0:T(8,128)S(1)}, u32[]{:S(2)}, u32[]{:S(2)}) collective-permute-start(f32[4,1,64,128]{3,2,1,0:T(8,128)S(1)} %get-tuple-element.78), channel_id=1, source_target_pairs={{0,4},{2,6},{4,0},{6,2},{8,12},{10,14},{12,8},{14,10},{16,20},{18,... | collective-permute-start | bytes 393224 | tf_op jit(solution)/shard_map/ppermute | solution.py:467
  56.1 5.0 %collective-permute-start.23 = (f32[4,1,64,128]{3,2,1,0:T(8,128)S(1)}, f32[4,1,64,128]{3,2,1,0:T(8,128)S(1)}, u32[]{:S(2)}, u32[]{:S(2)}) collective-permute-start(f32[4,1,64,128]{3,2,1,0:T(8,128)S(1)} %get-tuple-element.87), channel_id=1, source_target_pairs={{0,4},{2,6},{4,0},{6,2},{8,12},{10,14},{12,8},{14,10},{16,20},{18,... | collective-permute-start | bytes 393224 | tf_op jit(solution)/shard_map/ppermute | solution.py:467
  71.3 12.2 %all-to-all-start = ((f32[32,2,32]{2,1,0:T(2,128)}), f32[32,2,32]{2,1,0:T(2,128)S(1)}, u32[]{:S(2)}, u32[]{:S(2)}) async-start(f32[32,2,32]{2,1,0:T(2,128)} %broadcast_in_dim.34), calls=%async_computation | async-start | bytes 65536 | tf_op jit(solution)/shard_map/all_to_all | solution.py:524
  (14 other events, 29.3 us)

commit v2 on v1

v2 whole, which is shorter than its diff:
```python
import functools
import math

import jax
import jax.numpy as jnp
from jax import lax
from jax.experimental import pallas as pl
from jax.experimental.pallas import tpu as pltpu
from jax.sharding import PartitionSpec as P

F32 = jnp.float32
BF16 = jnp.bfloat16
LANES = 128
WIDE = 256
STATES = 64
RESETS = 8
CHUNKS = 4
ROOM = 16
NN = (((1,), (0,)), ((), ()))
NT = (((1,), (1,)), ((), ()))
TN = (((0,), (0,)), ((), ()))


def mm(a, b, dims=NN):
    return lax.dot_general(a, b, dims, preferred_element_type=F32)


def exact(a, b):
    return jnp.dot(a, b, precision=lax.Precision.HIGHEST, preferred_element_type=F32)


def halves(value):
    upper = value.astype(BF16)
    return upper, (value - upper.astype(F32)).astype(BF16)


def thirds(value):
    upper = value.astype(BF16)
    rest = value - upper.astype(F32)
    middle = rest.astype(BF16)
    return upper, middle, (rest - middle.astype(F32)).astype(BF16)


def iota(shape, dim):
    return lax.broadcasted_iota(jnp.int32, shape, dim)


def block_tables(deltas, log_rates, resets, first):
    length = deltas.shape[0]
    square = (length, length)
    row, col = iota(square, 0), iota(square, 1)
    lower = (row >= col).astype(F32)
    upper = (row <= col).astype(F32)
    rates = jnp.exp(log_rates)
    lam = -deltas * rates
    cum = exact(lower, lam)

    def marks(grid, ahead):
        hit = jnp.zeros(square, jnp.bool_)
        for k in range(RESETS):
            hit = hit | (grid + (first + ahead) == resets[0:1, k : k + 1])
        return hit.astype(BF16)

    low16, up16 = lower.astype(BF16), upper.astype(BF16)
    seg_f = mm(low16, marks(row, 0)), mm(marks(col, 0), up16)
    seg_r = mm(up16, marks(row, 1)), mm(marks(col, 1), low16)
    return rates, lam, cum, lower, upper, seg_f, seg_r


def expander(heads, width, start):
    shape = (3 * heads, width)
    per_head = 2 * LANES // 4
    return (iota(shape, 0) % heads == (iota(shape, 1) + start) // per_head).astype(BF16)


def spread_parts(values):
    return jnp.concatenate([jnp.concatenate(thirds(v), axis=1) for v in values], axis=0)


def factors(deltas, lam, cum):
    before = cum - lam
    return [deltas, jnp.exp(cum), jnp.exp(-cum), jnp.exp(-before), jnp.exp(before)]


def place_of(start, parts, chips):
    part, chip = divmod(start // WIDE, chips)
    return part // parts, part % parts, chip


class Packed:
    def __init__(self, pack_ref, heads, states):
        self.deltas = pack_ref[0:heads].T
        self.write = pack_ref[heads : heads + states].T.astype(BF16)
        self.read = pack_ref[heads + states : heads + 2 * states].T.astype(BF16)
        rows = heads + 2 * states
        self.log_rates = pack_ref[rows : rows + 1, 0:heads]
        self.skip = pack_ref[rows + 1 : rows + 2, 0:heads]
        self.resets = pack_ref[rows + 2 : rows + 3].astype(jnp.int32)


def states_kernel(chunks, chips, heads, states, x_hbm, cot_hbm, pack_ref, *refs):
    outs, (x_ref, cot_ref, wide_sem) = refs[: 2 * chunks], refs[2 * chunks :]
    length, channels = x_ref.shape
    starts = range(0, channels, WIDE)
    wides = [
        [
            pltpu.make_async_copy(source.at[:, pl.ds(start, WIDE)], target.at[:, pl.ds(start, WIDE)], wide_sem.at[i, start // WIDE])
            for i, (source, target) in enumerate(((x_hbm, x_ref), (cot_hbm, cot_ref)))
        ]
        for start in starts
    ]
    for both in wides:
        for copy in both:
            copy.start()
    index = lax.axis_index("seq")
    core = lax.rem(index, 2)
    given = Packed(pack_ref, heads, states)
    deltas = given.deltas
    rates, lam, cum, lower, upper, seg_f, seg_r = block_tables(deltas, given.log_rates, given.resets, index * length)
    seg_fc, seg_rc = seg_f[0][:, :states], seg_r[0][:, :states]
    write, read = given.write, given.read
    zero = jnp.zeros_like(write)
    write_f = jnp.where(seg_fc == seg_fc[length - 1 : length], write, zero)
    write_r = jnp.where(seg_rc == seg_rc[0:1], write, zero)
    read_f = jnp.where(seg_fc == 0.0, read, zero)
    read_r = jnp.where(seg_rc == 0.0, read, zero)
    open_f = jnp.where(seg_f[0][length - 1 : length, 0:1] == 0.0, 1.0, 0.0)
    open_r = jnp.where(seg_r[0][0:1, 0:1] == 0.0, 1.0, 0.0)
    parts = spread_parts(factors(deltas, lam, cum))
    keep, send = outs[:chunks], outs[chunks:]
    for start in starts:
        spread = mm(parts, expander(heads, WIDE, start))
        for copy in wides[start // WIDE]:
            copy.wait()
        step, u_f, v_f, u_r, v_r = (spread[i * length : (i + 1) * length] for i in range(5))
        lanes = slice(start, start + WIDE)
        scaled = (step * x_ref[:, lanes].astype(F32)).astype(BF16).astype(F32)
        cot = cot_ref[:, lanes].astype(F32)
        chain = u_f[length - 1 : length]
        carry_f = mm(write_f, (v_f * scaled).astype(BF16), TN) * chain
        carry_r = mm(write_r, (v_r * scaled).astype(BF16), TN)
        adj_f = mm(read_f, (u_f * cot).astype(BF16), TN)
        adj_r = mm(read_r, (u_r * cot).astype(BF16), TN) * chain
        tail = jnp.concatenate([open_f * chain, open_r * chain, jnp.zeros((6, WIDE), F32)], axis=0)
        chunk, part, chip = place_of(start, keep[0].shape[1], chips)
        rows = 0
        for value in (carry_f, adj_r, adj_f, carry_r, tail):
            zeroth, other = value[:, :LANES], value[:, LANES:]
            span = pl.ds(rows, value.shape[0])
            keep[chunk][chip, part, span] = jnp.where(core == 0, zeroth, other)
            send[chunk][chip, part, span] = jnp.where(core == 0, other, zeroth)
            rows += value.shape[0]


def position(chips):
    index = lax.axis_index("seq")
    core = lax.rem(index, 2)
    chip = lax.rem(lax.div(index, 2), chips)
    return core, chip, lax.div(index, 2 * chips)


def rows_of(scan):
    return pl.ds(scan * STATES, STATES)


def factor_of(ref, at, scan):
    return ref[(*at, pl.ds(4 * STATES + scan % 2, 1))]


def put_factors(ref, at, forward, reverse):
    ref[(*at, pl.ds(4 * STATES, 8))] = jnp.concatenate([forward, reverse, jnp.zeros((6, LANES), F32)], axis=0)


def chip_kernel(chips, keep_ref, got_ref, *outs):
    core, chip, _ = position(chips)
    for shift in range(chips):
        owner = lax.rem(chip + shift, chips)
        for part in range(keep_ref.shape[1]):
            at = (owner, part)
            for scan in range(4):
                mine, other = keep_ref[(*at, rows_of(scan))], got_ref[(*at, rows_of(scan))]
                own, far = factor_of(keep_ref, at, scan), factor_of(got_ref, at, scan)
                later = core == 1 if scan < 2 else core == 0
                outs[shift][part, rows_of(scan)] = jnp.where(later, mine + own * other, other + far * mine)
            both = [factor_of(keep_ref, at, scan) * factor_of(got_ref, at, scan) for scan in range(2)]
            put_factors(outs[shift], (part,), *both)


def plane_kernel(chips, _, *refs):
    gathered, out_ref = refs[:chips], refs[chips]
    _, chip, _ = position(chips)
    places = [lax.rem(chip + shift, chips) for shift in range(chips)]
    for part in range(out_ref.shape[0]):
        for scan in range(4):
            total = None
            for shift in range(chips):
                term = gathered[shift][part, rows_of(scan)]
                for other in range(chips):
                    if other != shift:
                        beyond = places[other] > places[shift] if scan < 2 else places[other] < places[shift]
                        term = jnp.where(beyond, factor_of(gathered[other], (part,), scan), 1.0) * term
                total = term if total is None else total + term
            out_ref[part, rows_of(scan)] = total
        products = [factor_of(gathered[0], (part,), scan) for scan in range(2)]
        for shift in range(1, chips):
            products = [products[scan] * factor_of(gathered[shift], (part,), scan) for scan in range(2)]
        put_factors(out_ref, (part,), *products)


def half_of(plane, level):
    return lax.rem(lax.shift_right_logical(plane, level), 2)


def hop_kernel(chips, level, last, *refs):
    (entered_ref, refs) = (refs[0], refs[1:]) if level > 0 else (None, refs)
    total_ref, got_ref, new_ref, onward_ref = refs
    _, _, plane = position(chips)
    bit, after = half_of(plane, level), half_of(plane, level + 1)
    for part in range(got_ref.shape[0]):
        totals, weights = [], []
        for scan in range(4):
            got, own = got_ref[part, rows_of(scan)], total_ref[part, rows_of(scan)]
            near, far = factor_of(total_ref, (part,), scan), factor_of(got_ref, (part,), scan)
            later = bit == 1 if scan < 2 else bit == 0
            if level > 0:
                entered, weight = entered_ref[part, rows_of(scan)], entered_ref[part, pl.ds(4 * STATES + scan, 1)]
            else:
                entered, weight = jnp.zeros_like(got), jnp.ones_like(far)
            new_ref[part, rows_of(scan)] = jnp.where(later, entered + weight * got, entered)
            weights.append(jnp.where(later, weight * far, weight))
            totals.append(jnp.where(later, own + near * got, got + far * own))
        new_ref[part, pl.ds(4 * STATES, 8)] = jnp.concatenate(weights + [jnp.zeros((4, LANES), F32)], axis=0)
        if last:
            for scan in range(2):
                onward_ref[part, rows_of(scan)] = jnp.where(after == 0, totals[scan], totals[scan + 2])
        else:
            for scan in range(4):
                onward_ref[part, rows_of(scan)] = totals[scan]
            both = [factor_of(total_ref, (part,), scan) * factor_of(got_ref, (part,), scan) for scan in range(2)]
            put_factors(onward_ref, (part,), *both)


def spread_kernel(chips, level, entered_ref, got_ref, *refs):
    gathered, outs = refs[:chips], refs[chips:]
    _, chip, plane = position(chips)
    bit = half_of(plane, level)
    places = [lax.rem(chip + shift, chips) for shift in range(chips)]
    for part in range(got_ref.shape[0]):
        for scan in range(4):
            weight = entered_ref[part, pl.ds(4 * STATES + scan, 1)]
            later = bit == 1 if scan < 2 else bit == 0
            value = entered_ref[part, rows_of(scan)]
            value = jnp.where(later, value + weight * got_ref[part, rows_of(scan % 2)], value)
            whole = [factor_of(gathered[shift], (part,), scan) for shift in range(chips)]

            def before(a, b):
                return places[a] < places[b] if scan < 2 else places[a] > places[b]

            for target in range(chips):
                total = value
                for other in range(chips):
                    if other != target:
                        total = jnp.where(before(other, target), whole[other], 1.0) * total
                for source in range(chips):
                    if source == target:
                        continue
                    term = gathered[source][part, rows_of(scan)]
                    for other in range(chips):
                        if other not in (source, target):
                            between = before(source, other) & before(other, target)
                            term = jnp.where(between, whole[other], 1.0) * term
                    total = jnp.where(before(source, target), total + term, total)
                outs[target][part, rows_of(scan)] = total


def core_kernel(chips, keep_ref, got_ref, *refs):
    entered, (own_ref, send_ref) = refs[:chips], refs[chips:]
    core, chip, _ = position(chips)
    for shift in range(chips):
        owner = lax.rem(chip + chips - shift, chips)
        for part in range(keep_ref.shape[1]):
            at = (owner, part)
            for scan in range(4):
                value = entered[shift][part, rows_of(scan)]
                mine, other = keep_ref[(*at, rows_of(scan))], got_ref[(*at, rows_of(scan))]
                near = core == 0 if scan < 2 else core == 1
                to_own = factor_of(got_ref, at, scan) * value + other
                to_other = factor_of(keep_ref, at, scan) * value + mine
                own_ref[(*at, rows_of(scan))] = jnp.where(near, value, to_own)
                send_ref[(*at, rows_of(scan))] = jnp.where(near, to_other, value)


class Block:
    def __init__(self, given):
        deltas, write, read = given.deltas, given.write, given.read
        length, states = deltas.shape[0], write.shape[1]
        tables = block_tables(deltas, given.log_rates, given.resets, lax.axis_index("seq") * length)
        self.rates, self.lam, self.cum, self.lower, self.upper, seg_f, seg_r = tables
        self.mask_f = (self.lower > 0.0) & (seg_f[0] == seg_f[1])
        self.mask_r = (self.upper > 0.0) & (seg_r[0] == seg_r[1])
        seg_fc, seg_rc = seg_f[0][:, :states], seg_r[0][:, :states]
        self.end_f, self.end_r = seg_fc == seg_fc[length - 1 : length], seg_rc == seg_rc[0:1]
        self.start_f, self.start_r = seg_fc == 0.0, seg_rc == 0.0
        zero = jnp.zeros_like(write)
        self.write, self.read = write, read
        self.write_f, self.write_r = jnp.where(self.end_f, write, zero), jnp.where(self.end_r, write, zero)
        self.read_f, self.read_r = jnp.where(self.start_f, read, zero), jnp.where(self.start_r, read, zero)
        self.open_f = jnp.where(seg_f[0][length - 1 : length, 0:1] == 0.0, 1.0, 0.0)
        self.open_r = jnp.where(seg_r[0][0:1, 0:1] == 0.0, 1.0, 0.0)


def reduced(flows, collect):
    high, low = halves(flows)
    return mm(high, collect, NT) + mm(low, collect, NT)


def inner_kernel(heads, states, x_ref, cot_ref, pack_ref, *outs):
    y_ref, g_ref, flow_ref, gread_ref, gwrite_ref, rate_ref = outs[-6:]
    length, channels = x_ref.shape
    given = Packed(pack_ref, heads, states)
    deltas, own = given.deltas, Block(given)
    scores = mm(own.read, own.write, NT)
    scores_f = jnp.where(own.mask_f, scores, 0.0).astype(BF16)
    scores_r = jnp.where(own.mask_r, scores, 0.0).astype(BF16)
    parts = spread_parts(factors(deltas, own.lam, own.cum) + [own.cum, own.cum - own.lam])
    flow = jnp.zeros((3 * length, heads), F32)
    pair_f = jnp.zeros((length, length), F32)
    pair_r = jnp.zeros((length, length), F32)
    for start in range(0, channels, WIDE):
        expand = expander(heads, WIDE, start)
        spread = mm(parts, expand)
        step, u_f, v_f, u_r, v_r, cum, before = (spread[i * length : (i + 1) * length] for i in range(7))
        lanes = slice(start, start + WIDE)
        x = x_ref[:, lanes].astype(F32)
        cot = cot_ref[:, lanes].astype(F32)
        scaled = (step * x).astype(BF16).astype(F32)
        whole, chain = cum[length - 1 : length], u_f[length - 1 : length]
        wide_sf, wide_sr, wide_cf, wide_cr = v_f * scaled, v_r * scaled, u_f * cot, u_r * cot
        sc_f, sc_r, ct_f, ct_r = (value.astype(BF16) for value in (wide_sf, wide_sr, wide_cf, wide_cr))
        pre_f, pre_r = mm(scores_f, sc_f), mm(scores_r, sc_r)
        y_f, y_r = u_f * pre_f, u_r * pre_r
        g_f, g_r = v_f * mm(scores_f, ct_f, TN), v_r * mm(scores_r, ct_r, TN)
        grad = g_f + g_r
        y_ref[:, lanes] = (y_f + y_r).astype(BF16)
        g_ref[:, lanes] = grad.astype(BF16)
        flow = flow + reduced(jnp.concatenate([cot * y_f - scaled * g_f, cot * y_r - scaled * g_r, x * grad], axis=0), expand[:heads])
        pair_f = pair_f + mm(ct_f, sc_f, NT)
        pair_r = pair_r + mm(ct_r, sc_r, NT)
        from_end = whole - cum
        centre, centre_r = cum - 0.5 * whole, before - 0.5 * whole
        within = centre * wide_cf * pre_f - wide_cf * mm(scores_f, (centre * wide_sf).astype(BF16))
        within = within + wide_cr * mm(scores_r, (centre_r * wide_sr).astype(BF16)) - centre_r * wide_cr * pre_r
        at = start // WIDE
        rate_ref[at, 0:states] = mm(own.read_f, (cum * wide_cf).astype(BF16), TN)
        rate_ref[at, states : 2 * states] = mm(own.write_r, (before * wide_sr).astype(BF16), TN)
        rate_ref[at, 2 * states : 3 * states] = mm(own.write_f, (from_end * wide_sf).astype(BF16), TN) * chain
        rate_ref[at, 3 * states : 4 * states] = mm(own.read_r, ((whole - before) * wide_cr).astype(BF16), TN) * chain
        tail = [own.open_f * chain * whole, own.open_r * chain * whole, jnp.sum(within, axis=0, keepdims=True)]
        tail = tail + [jnp.sum(x * cot, axis=0, keepdims=True), jnp.zeros((4, WIDE), F32)]
        rate_ref[at, 4 * states : 4 * states + 8] = jnp.concatenate(tail, axis=0)
    pairs = (jnp.where(own.mask_f, pair_f, 0.0) + jnp.where(own.mask_r, pair_r, 0.0)).astype(BF16)
    gread_ref[...] = mm(pairs, own.write)
    gwrite_ref[...] = mm(pairs, own.read, TN)
    flow_ref[...] = flow


def entering_states(own, got, start, chips):
    core = lax.rem(lax.axis_index("seq"), 2)
    chunk, part, chip = place_of(start, own[0].shape[1], chips)
    values = []
    for scan in range(4):
        a, b = own[chunk][chip, part, rows_of(scan)], got[chunk][chip, part, rows_of(scan)]
        values.append(jnp.concatenate([jnp.where(core == 0, a, b), jnp.where(core == 0, b, a)], axis=1))
    return values


def rates_kernel(chunks, chips, rate_ref, *refs):
    own, got, small_ref = refs[:chunks], refs[chunks : 2 * chunks], refs[2 * chunks]
    heads = small_ref.shape[1]
    total = jnp.zeros((8, heads), F32)
    for at in range(rate_ref.shape[0]):
        in_f, back_r, back_f, in_r = entering_states(own, got, at * WIDE, chips)
        tail = rate_ref[at, pl.ds(4 * STATES, 8)]
        met = sum(value * rate_ref[at, rows_of(scan)] for scan, value in enumerate((in_f, back_r, back_f, in_r)))
        met = met + tail[0:1] * (in_f * back_f) + tail[1:2] * (in_r * back_r)
        met = jnp.sum(met, axis=0, keepdims=True) + tail[2:3]
        rows = jnp.concatenate([met, tail[3:4], jnp.zeros((6, WIDE), F32)], axis=0)
        collect = expander(heads, WIDE, at * WIDE)[:heads]
        for piece in thirds(rows):
            total = total + mm(piece, collect, NT)
    small_ref[...] = total[:2]


def finish_kernel(chunks, chips, heads, states, x_ref, cot_ref, pack_ref, *refs):
    y_ref, g_ref, flow_ref, gread0_ref, gwrite0_ref = refs[:5]
    entered, got = refs[5 : 5 + chunks], refs[5 + chunks : 5 + 2 * chunks]
    out_ref, gin_ref, steps_ref, gwrite_ref, gread_ref = refs[5 + 2 * chunks :]
    length, channels = x_ref.shape
    given = Packed(pack_ref, heads, states)
    deltas, own = given.deltas, Block(given)
    skip = jnp.broadcast_to(given.skip, (8, heads))
    parts = spread_parts(factors(deltas, own.lam, own.cum) + [skip])
    flow = flow_ref[...]
    rows = jnp.zeros((8, heads), F32)
    acc_read_f = jnp.zeros((length, states), F32)
    acc_read_r = jnp.zeros((length, states), F32)
    acc_write_f = jnp.zeros((length, states), F32)
    acc_write_r = jnp.zeros((length, states), F32)
    for start in range(0, channels, WIDE):
        expand = expander(heads, WIDE, start)
        spread = mm(parts, expand)
        step, u_f, v_f, u_r, v_r = (spread[i * length : (i + 1) * length] for i in range(5))
        gain = spread[5 * length : 5 * length + 1]
        lanes = slice(start, start + WIDE)
        x = x_ref[:, lanes].astype(F32)
        cot = cot_ref[:, lanes].astype(F32)
        scaled = (step * x).astype(BF16).astype(F32)
        chain = u_f[length - 1 : length]
        sc_f, sc_r = (v_f * scaled).astype(BF16), (v_r * scaled).astype(BF16)
        ct_f, ct_r = (u_f * cot).astype(BF16), (u_r * cot).astype(BF16)
        in_f, back_r, back_f, in_r = entering_states(entered, got, start, chips)
        in_f16, in_r16 = in_f.astype(BF16), (in_r * chain).astype(BF16)
        back_f16, back_r16 = (back_f * chain).astype(BF16), back_r.astype(BF16)
        y_f, y_r = u_f * mm(own.read_f, in_f16), u_r * mm(own.read_r, in_r16)
        g_f, g_r = v_f * mm(own.write_f, back_f16), v_r * mm(own.write_r, back_r16)
        out_ref[:, lanes] = (y_ref[:, lanes] + (y_f + y_r) + gain * x).astype(BF16)
        grad = g_f + g_r
        gin_ref[:, lanes] = (step * (g_ref[:, lanes] + grad) + gain * cot).astype(BF16)
        local_f, local_r = mm(own.write_f, sc_f, TN) * chain, mm(own.write_r, sc_r, TN)
        through = back_f * (local_f + own.open_f * chain * in_f) + back_r * (local_r + own.open_r * chain * in_r)
        through = jnp.sum(through, axis=0, keepdims=True)
        small = jnp.concatenate([through, jnp.zeros((7, WIDE), F32)], axis=0)
        sums = reduced(jnp.concatenate([cot * y_f - scaled * g_f, cot * y_r - scaled * g_r, x * grad, small], axis=0), expand[:heads])
        flow = flow + sums[: 3 * length]
        rows = rows + sums[3 * length :]
        acc_read_f = acc_read_f + mm(ct_f, in_f16, NT)
        acc_read_r = acc_read_r + mm(ct_r, in_r16, NT)
        acc_write_f = acc_write_f + mm(sc_f, back_f16, NT)
        acc_write_r = acc_write_r + mm(sc_r, back_r16, NT)
    gread = gread0_ref[...] + jnp.where(own.start_f, acc_read_f, 0.0) + jnp.where(own.start_r, acc_read_r, 0.0)
    gwrite = gwrite0_ref[...] + jnp.where(own.end_f, acc_write_f, 0.0) + jnp.where(own.end_r, acc_write_r, 0.0)
    gread_ref[...] = gread.T
    gwrite_ref[...] = gwrite.T
    logs = exact(own.upper, flow[:length]) + exact(own.lower, flow[length : 2 * length]) + rows[0:1]
    steps_ref[...] = (flow[2 * length :] - own.rates * logs).T


def call(body, out_shape, spaces, flops, size, name, scratch=(), room=16):
    return pl.pallas_call(
        body,
        out_shape=out_shape,
        in_specs=[pl.BlockSpec(memory_space=space) for space in spaces],
        out_specs=jax.tree.map(lambda _: pl.BlockSpec(memory_space=pltpu.VMEM), out_shape),
        scratch_shapes=scratch,
        compiler_params=pltpu.CompilerParams(vmem_limit_bytes=room << 20),
        cost_estimate=pl.CostEstimate(flops=flops, bytes_accessed=size, transcendentals=0),
        name=name,
    )


def local(chips, inputs, step_sizes, write_vecs, read_vecs, log_rates, skip_gain, resets, cotangent):
    x, cot = inputs[0], cotangent[0]
    deltas, write, read = step_sizes[0].T, write_vecs[0].T, read_vecs[0].T
    length, channels = x.shape
    heads, states = deltas.shape[0], write.shape[0]
    devices = lax.axis_size("seq")
    planes = devices // (2 * chips)
    levels = int(math.log2(planes))
    chunks = min(CHUNKS, channels // (WIDE * chips))
    parts = channels // (WIDE * chips * chunks)
    lined = [jnp.pad(row.astype(F32)[None], ((0, 0), (0, length - row.shape[0]))) for row in (log_rates, skip_gain, resets[0])]
    pack = jnp.concatenate([deltas, write.astype(F32), read.astype(F32), *lined, jnp.zeros((5, length), F32)], axis=0)

    def like(*shape, kind=F32):
        return jax.ShapeDtypeStruct(shape, kind)

    vmem = pltpu.VMEM
    message, plain = 4 * states + 8, 4 * states
    group = like(chips, parts, message, LANES)
    single = like(parts, message, LANES)
    half = like(parts, 2 * states, LANES)
    bare = like(parts, plain, LANES)
    pair = like(chips, parts, plain, LANES)
    made = call(
        functools.partial(states_kernel, chunks, chips, heads, states),
        [group] * (2 * chunks),
        [pl.ANY] * 2 + [vmem],
        300 * 10**6,
        4 * 10**6,
        "states",
        [
            pltpu.VMEM((length, channels), BF16),
            pltpu.VMEM((length, channels), BF16),
            pltpu.SemaphoreType.DMA((2, channels // WIDE)),
        ],
        ROOM,
    )(x, cot, pack)
    keep, send = made[:chunks], made[chunks:]

    def device(plane, chip, core):
        return (plane * chips + chip) * 2 + core

    every = [(p, a, c) for p in range(planes) for a in range(chips) for c in range(2)]
    swap = [(device(p, a, c), device(p, a, 1 - c)) for p, a, c in every]

    def turn(shift):
        return [(device(p, a, c), device(p, (a + shift) % chips, c)) for p, a, c in every]

    def across(level):
        return [(device(p, a, c), device(p ^ 2**level, a, c)) for p, a, c in every]

    def send_to(value, perm):
        return lax.ppermute(value, "seq", perm)

    gots, chipped = [], []
    for k in range(chunks):
        gots.append(send_to(send[k], swap))
        chipped.append(call(functools.partial(chip_kernel, chips), [single] * chips, [vmem] * 2, 10**6, 10**6, "chip")(keep[k], gots[k]))
    inner = call(
        functools.partial(inner_kernel, heads, states),
        [
            like(length, channels, kind=BF16),
            like(length, channels, kind=BF16),
            like(3 * length, heads),
            like(length, states),
            like(length, states),
            like(channels // WIDE, message, WIDE),
        ],
        [vmem] * 3 + [pl.ANY] * chunks,
        10**9,
        8 * 10**6,
        "inner",
    )(x, cot, pack, *[value[0] for value in chipped])
    size = 4 * parts * states * LANES * 4
    owns, theirs_in = [], []
    for k in range(chunks):
        got, chip_totals = gots[k], chipped[k]
        gathered = [chip_totals[0]] + [None] * (chips - 1)
        for shift in range(1, chips):
            gathered[chips - shift] = send_to(chip_totals[shift], turn(shift))
        onward = call(functools.partial(plane_kernel, chips), single, [pl.ANY] + [vmem] * chips, 10**6, size * 3, "plane")(inner[3], *gathered)
        before = []
        for level in range(levels - 1):
            arrived = send_to(onward, across(level))
            last = level == levels - 2
            hop = call(
                functools.partial(hop_kernel, chips, level, last),
                [single, half if last else single],
                [vmem] * (2 + len(before)),
                10**6,
                size * 4,
                "hop",
            )
            entry, onward = hop(*before, onward, arrived)
            before = [entry]
        arrived = send_to(onward, across(levels - 1))
        placed = call(
            functools.partial(spread_kernel, chips, levels - 1), [bare] * chips, [vmem] * (2 + chips), 10**6, size * 5, "spread"
        )(*before, arrived, *gathered)
        entered = [placed[0]] + [send_to(placed[shift], turn(shift)) for shift in range(1, chips)]
        mine, theirs = call(functools.partial(core_kernel, chips), [pair] * 2, [vmem] * (2 + chips), 10**6, size * 8, "core")(
            keep[k], got, *entered
        )
        owns.append(mine)
        theirs_in.append(send_to(theirs, swap))

    small = call(
        functools.partial(rates_kernel, chunks, chips), like(2, heads), [vmem] * (1 + 2 * chunks), 10**6, 4 * 10**6, "rates"
    )(inner[5], *owns, *theirs_in)
    count = devices * lax.axis_size("dp")
    copies = jnp.broadcast_to(small[None], (count,) + small.shape)
    total = jnp.sum(lax.all_to_all(copies, ("seq", "dp"), 0, 0, tiled=True), axis=0)
    outputs, grad_inputs, grad_steps, grad_write, grad_read = call(
        functools.partial(finish_kernel, chunks, chips, heads, states),
        [
            like(length, channels, kind=BF16),
            like(length, channels, kind=BF16),
            like(heads, length),
            like(states, length),
            like(states, length),
        ],
        [vmem] * (8 + 2 * chunks),
        2 * 10**9,
        6 * 10**6,
        "finish",
    )(x, cot, pack, *inner[:5], *owns, *theirs_in)
    return (outputs[None], grad_inputs[None], grad_steps.T[None], grad_write.T[None], grad_read.T[None], total[0], total[1])


def solution(mesh):
    along = P("dp", "seq", None)
    chips = 2 ** (int(math.log2(mesh.shape["seq"] // 2)) // 2)
    return jax.shard_map(
        functools.partial(local, chips),
        mesh=mesh,
        in_specs=(along, along, along, along, P(), P(), P("dp", None), along),
        out_specs=(along, along, along, along, along, P(), P()),
        check_vma=False,
    )
```

time: 84.4 us -> 69.9 us (0.83)
  Pallas kernels: 26.2 us -> 16.1 us
  starting transfers between devices: 36.3 us -> 31.7 us
  waiting for transfers between devices: 12.7 us -> 11 us
  other arithmetic: 0.07 us -> 1.44 us
    pallas_call x23 -> x24, Pallas kernels: 26.2 us -> 16.1 us  [the longest x1 5.56 us: local(): call(functools.partial(finish_kernel, chunks, chips, heads, states), [lik...]
    ppermute x4 -> x0, starting transfers between devices: 8.72 us -> none  [local(): far = lax.ppermute(table, 'seq', [(i, i ^ reach) for i in range(devices)])]
    ppermute x24, waiting for transfers between devices: 2.73 us -> 11 us  [send_to(): return lax.ppermute(value, 'seq', perm)]
    all_to_all x1, waiting for transfers between devices: 5.27 us -> 0.01 us  [local(): lax.all_to_all(copies, ('seq', 'dp'), 0, 0, tiled=True)]
    ppermute x4 -> x0, waiting for transfers between devices: 4.7 us -> none  [local(): far = lax.ppermute(table, 'seq', [(i, i ^ reach) for i in range(devices)])]
    ppermute x24, starting transfers between devices: 22.8 us -> 26.2 us  [send_to(): return lax.ppermute(value, 'seq', perm)]
    unnamed x24 -> x20, local copies, waits for them, and re-layouts: 6.65 us -> 5.02 us
    convert_element_type x0 -> x2, other arithmetic: none -> 1.4 us  [the longest x1 0.74 us: local(): read.astype(F32)]
  transfers between devices with their start and end apart: 29 -> 25, of which waited for: 6 -> 11; matrix products, arithmetic and copies ran while one was open for 3% -> 0% of each run, Pallas kernels for 23% -> 17%
where the time goes in v2:
time: 69.9 us; the launch traced here: 69.4 us
  starting transfers between devices  31.7 us (45%)
  Pallas kernels  16.1 us (23%)
  waiting for transfers between devices  11 us (16%)
  local copies, waits for them, and re-layouts  8.25 us (12%)
  other arithmetic  1.44 us (2%)
  between operations  0.89 us (1%)
    ppermute x24, starting transfers between devices, send_to(): return lax.ppermute(value, 'seq', perm)  26.2 us
    ppermute x24, waiting for transfers between devices, send_to(): return lax.ppermute(value, 'seq', perm)  11 us
    pallas_call x1, Pallas kernels, local(): call(functools.partial(finish_kernel, chunks, chips, heads, states), [lik...  5.56 us
    all_to_all x1, starting transfers between devices, local(): lax.all_to_all(copies, ('seq', 'dp'), 0, 0, tiled=True)  5.49 us
    unnamed x20, local copies, waits for them, and re-layouts  5.02 us
    pallas_call x1, Pallas kernels, local(): call(functools.partial(inner_kernel, heads, states), [like(length, channe...  4.98 us
    pallas_call x1, Pallas kernels, local(): call(functools.partial(states_kernel, chunks, chips, heads, states), [gro...  3.98 us
  transfers between devices with their start and end apart: 25, of which 11 were waited for; matrix products, arithmetic and copies ran while one was open for 0% of the time, Pallas kernels for 17%

profile of v2, /device:TPU:0, one launch (start us, length us, event | category | flops | bytes accessed | tf_op | source)
XLA Modules:
  0.0 69.4 jit_solution(11677475800863277211)
XLA Ops:
  4.1 1.0 %copy-done = bf16[1,128,2048]{2,1,0:T(8,128)(2,1)S(1)} copy-done((bf16[1,128,2048]{2,1,0:T(8,128)(2,1)S(1)}, bf16[1,128,2048]{2,1,0:T(8,128)(2,1)}, u32[]{:S(2)}) %copy-start) | copy-done | bytes 524312
  5.2 1.0 %copy-done.2 = bf16[1,128,2048]{2,1,0:T(8,128)(2,1)S(1)} copy-done((bf16[1,128,2048]{2,1,0:T(8,128)(2,1)S(1)}, bf16[1,128,2048]{2,1,0:T(8,128)(2,1)}, u32[]{:S(2)}) %copy-start.2) | copy-done | bytes 524312
  6.2 4.0 %states.1 = (f32[2,1,264,128]{3,2,1,0:T(8,128)S(1)}, f32[2,1,264,128]{3,2,1,0:T(8,128)S(1)}, f32[2,1,264,128]{3,2,1,0:T(8,128)S(1)}, f32[2,1,264,128]{3,2,1,0:T(...) custom-call(bf16[128,2048]{1,0:T(8,128)(2,1)S(1)} %bitcast.32, ...), custom_call_target="tpu_custom_call" | custom-call | flops 300000000 | bytes 4000000 | tf_op jit(solution)/shard_map/states/pallas_call | solution.py:484
  11.9 2.9 %collective-permute-start.16 = (f32[1,264,128]{2,1,0:T(8,128)S(1)}, f32[1,264,128]{2,1,0:T(8,128)S(1)}, u32[]{:S(2)}, u32[]{:S(2)}) collective-permute-start(f32[1,264,128]{2,1,0:T(8,128)S(1)} %get-tuple-element.93), channel_id=1, source_target_pairs={{0,4},{2,6},{4,0},{6,2},{8,12},{10,14},{12,8},{14,10},{16,20},{18,... | collective-permute-start | bytes 405512 | tf_op jit(solution)/shard_map/ppermute | solution.py:513
  15.3 1.8 %collective-permute-start.8 = (f32[1,264,128]{2,1,0:T(8,128)S(1)}, f32[1,264,128]{2,1,0:T(8,128)S(1)}, u32[]{:S(2)}, u32[]{:S(2)}) collective-permute-start(f32[1,264,128]{2,1,0:T(8,128)S(1)} %get-tuple-element.81), channel_id=1, source_target_pairs={{0,4},{2,6},{4,0},{6,2},{8,12},{10,14},{12,8},{14,10},{16,20},{18,... | collective-permute-start | bytes 405512 | tf_op jit(solution)/shard_map/ppermute | solution.py:513
  17.5 5.0 %inner.1 = (bf16[128,2048]{1,0:T(8,128)(2,1)S(1)}, bf16[128,2048]{1,0:T(8,128)(2,1)S(1)}, f32[384,32]{1,0:T(8,128)S(1)}, f32[128,64]{1,0:T(8,128)S(1)}, f32[128,...) custom-call(bf16[128,2048]{1,0:T(8,128)(2,1)S(1)} %bitcast.33, bf16[128,2048]{1,0:T(8,128)(2,1)S(1)} %bitcast.36, ...), custom_call_target="tpu_custom_call" | custom-call | flops 1000000000 | bytes 8000000 | tf_op jit(solution)/shard_map/inner/pallas_call | solution.py:519
  22.6 1.9 %collective-permute-start.17 = (f32[1,264,128]{2,1,0:T(8,128)S(1)}, f32[1,264,128]{2,1,0:T(8,128)S(1)}, u32[]{:S(2)}, u32[]{:S(2)}) collective-permute-start(f32[1,264,128]{2,1,0:T(8,128)S(1)} %plane.7.refs_0_), channel_id=1, source_target_pairs={{0,8},{2,10},{4,12},{6,14},{8,0},{10,2},{12,4},{14,6},{16,24},{18,... | collective-permute-start | bytes 405512 | tf_op jit(solution)/shard_map/ppermute | solution.py:513
  25.0 2.2 %collective-permute-start.9 = (f32[1,264,128]{2,1,0:T(8,128)S(1)}, f32[1,264,128]{2,1,0:T(8,128)S(1)}, u32[]{:S(2)}, u32[]{:S(2)}) collective-permute-start(f32[1,264,128]{2,1,0:T(8,128)S(1)} %plane.5.refs_0_), channel_id=1, source_target_pairs={{0,8},{2,10},{4,12},{6,14},{8,0},{10,2},{12,4},{14,6},{16,24},{18,... | collective-permute-start | bytes 405512 | tf_op jit(solution)/shard_map/ppermute | solution.py:513
  27.5 1.9 %collective-permute-start.5 = (f32[1,264,128]{2,1,0:T(8,128)S(1)}, f32[1,264,128]{2,1,0:T(8,128)S(1)}, u32[]{:S(2)}, u32[]{:S(2)}) collective-permute-start(f32[1,264,128]{2,1,0:T(8,128)S(1)} %plane.4.refs_0_), channel_id=1, source_target_pairs={{0,8},{2,10},{4,12},{6,14},{8,0},{10,2},{12,4},{14,6},{16,24},{18,... | collective-permute-start | bytes 405512 | tf_op jit(solution)/shard_map/ppermute | solution.py:513
  29.4 2.8 %collective-permute-start.18 = (f32[1,128,128]{2,1,0:T(8,128)S(1)}, f32[1,128,128]{2,1,0:T(8,128)S(1)}, u32[]{:S(2)}, u32[]{:S(2)}) collective-permute-start(f32[1,128,128]{2,1,0:T(8,128)S(1)} %get-tuple-element.95), channel_id=1, source_target_pairs={{0,16},{2,18},{4,20},{6,22},{8,24},{10,26},{12,28},{14,30},{16,0},... | collective-permute-start | bytes 196616 | tf_op jit(solution)/shard_map/ppermute | solution.py:513
  32.2 3.4 %collective-permute-start.14 = (f32[1,128,128]{2,1,0:T(8,128)S(1)}, f32[1,128,128]{2,1,0:T(8,128)S(1)}, u32[]{:S(2)}, u32[]{:S(2)}) collective-permute-start(f32[1,128,128]{2,1,0:T(8,128)S(1)} %get-tuple-element.89), channel_id=1, source_target_pairs={{0,16},{2,18},{4,20},{6,22},{8,24},{10,26},{12,28},{14,30},{16,0},... | collective-permute-start | bytes 196616 | tf_op jit(solution)/shard_map/ppermute | solution.py:513
  35.6 2.3 %collective-permute-done.9.refs_1_ = f32[1,264,128]{2,1,0:T(8,128)S(1)} collective-permute-done((f32[1,264,128]{2,1,0:T(8,128)S(1)}, f32[1,264,128]{2,1,0:T(8,128)S(1)}, u32[]{:S(2)}, u32[]{:S(2)}) %collective-permute-start.9) | collective-permute-done | bytes 135200 | tf_op jit(solution)/shard_map/ppermute | solution.py:513
  37.9 1.4 %collective-permute-start.10 = (f32[1,128,128]{2,1,0:T(8,128)S(1)}, f32[1,128,128]{2,1,0:T(8,128)S(1)}, u32[]{:S(2)}, u32[]{:S(2)}) collective-permute-start(f32[1,128,128]{2,1,0:T(8,128)S(1)} %get-tuple-element.83), channel_id=1, source_target_pairs={{0,16},{2,18},{4,20},{6,22},{8,24},{10,26},{12,28},{14,30},{16,0},... | collective-permute-start | bytes 196616 | tf_op jit(solution)/shard_map/ppermute | solution.py:513
  39.7 1.3 %collective-permute-start.6 = (f32[1,128,128]{2,1,0:T(8,128)S(1)}, f32[1,128,128]{2,1,0:T(8,128)S(1)}, u32[]{:S(2)}, u32[]{:S(2)}) collective-permute-start(f32[1,128,128]{2,1,0:T(8,128)S(1)} %get-tuple-element.77), channel_id=1, source_target_pairs={{0,16},{2,18},{4,20},{6,22},{8,24},{10,26},{12,28},{14,30},{16,0},... | collective-permute-start | bytes 196616 | tf_op jit(solution)/shard_map/ppermute | solution.py:513
  41.1 1.4 %collective-permute-start.19 = (f32[1,256,128]{2,1,0:T(8,128)S(1)}, f32[1,256,128]{2,1,0:T(8,128)S(1)}, u32[]{:S(2)}, u32[]{:S(2)}) collective-permute-start(f32[1,256,128]{2,1,0:T(8,128)S(1)} %get-tuple-element.97), channel_id=1, source_target_pairs={{0,4},{2,6},{4,0},{6,2},{8,12},{10,14},{12,8},{14,10},{16,20},{18,... | collective-permute-start | bytes 393224 | tf_op jit(solution)/shard_map/ppermute | solution.py:513
  43.3 1.1 %collective-permute-done.10.got_ref = f32[1,128,128]{2,1,0:T(8,128)S(1)} collective-permute-done((f32[1,128,128]{2,1,0:T(8,128)S(1)}, f32[1,128,128]{2,1,0:T(8,128)S(1)}, u32[]{:S(2)}, u32[]{:S(2)}) %collective-permute-start.10) | collective-permute-done | bytes 65568 | tf_op jit(solution)/shard_map/ppermute | solution.py:513
  44.6 1.6 %collective-permute-start.11 = (f32[1,256,128]{2,1,0:T(8,128)S(1)}, f32[1,256,128]{2,1,0:T(8,128)S(1)}, u32[]{:S(2)}, u32[]{:S(2)}) collective-permute-start(f32[1,256,128]{2,1,0:T(8,128)S(1)} %get-tuple-element.85), channel_id=1, source_target_pairs={{0,4},{2,6},{4,0},{6,2},{8,12},{10,14},{12,8},{14,10},{16,20},{18,... | collective-permute-start | bytes 393224 | tf_op jit(solution)/shard_map/ppermute | solution.py:513
  47.0 1.1 %collective-permute-done.15.refs_1_ = f32[1,256,128]{2,1,0:T(8,128)S(1)} collective-permute-done((f32[1,256,128]{2,1,0:T(8,128)S(1)}, f32[1,256,128]{2,1,0:T(8,128)S(1)}, u32[]{:S(2)}, u32[]{:S(2)}) %collective-permute-start.15) | collective-permute-done | bytes 131104 | tf_op jit(solution)/shard_map/ppermute | solution.py:513
  48.3 2.2 %collective-permute-done.11.refs_1_ = f32[1,256,128]{2,1,0:T(8,128)S(1)} collective-permute-done((f32[1,256,128]{2,1,0:T(8,128)S(1)}, f32[1,256,128]{2,1,0:T(8,128)S(1)}, u32[]{:S(2)}, u32[]{:S(2)}) %collective-permute-start.11) | collective-permute-done | bytes 131104 | tf_op jit(solution)/shard_map/ppermute | solution.py:513
  50.7 1.3 %collective-permute-done.7.refs_1_ = f32[1,256,128]{2,1,0:T(8,128)S(1)} collective-permute-done((f32[1,256,128]{2,1,0:T(8,128)S(1)}, f32[1,256,128]{2,1,0:T(8,128)S(1)}, u32[]{:S(2)}, u32[]{:S(2)}) %collective-permute-start.7) | collective-permute-done | bytes 131104 | tf_op jit(solution)/shard_map/ppermute | solution.py:513
  52.2 1.4 %collective-permute-done.20.refs_9_.refs_4_ = f32[2,1,256,128]{3,2,1,0:T(8,128)S(1)} collective-permute-done((f32[2,1,256,128]{3,2,1,0:T(8,128)S(1)}, f32[2,1,256,128]{3,2,1,0:T(8,128)S(1)}, u32[]{:S(2)}, u32[]{:S(2)}) %collective-permute-start.20) | collective-permute-done | bytes 262176 | tf_op jit(solution)/shard_map/ppermute | solution.py:513
  54.8 5.5 %all-to-all-start = ((f32[32,2,32]{2,1,0:T(2,128)}), f32[32,2,32]{2,1,0:T(2,128)S(1)}, u32[]{:S(2)}, u32[]{:S(2)}) async-start(f32[32,2,32]{2,1,0:T(2,128)} %broadcast_in_dim.39), calls=%async_computation | async-start | bytes 65536 | tf_op jit(solution)/shard_map/all_to_all | solution.py:572
  61.4 1.0 %copy-done.7 = bf16[128,2048]{1,0:T(8,128)(2,1)S(1)} copy-done((bf16[128,2048]{1,0:T(8,128)(2,1)S(1)}, bf16[128,2048]{1,0:T(8,128)(2,1)}, u32[]{:S(2)}) %copy-start.7) | copy-done | bytes 524312
  63.3 5.6 %finish.1 = (bf16[128,2048]{1,0:T(8,128)(2,1)}, bf16[128,2048]{1,0:T(8,128)(2,1)}, f32[32,128]{1,0:T(8,128)}, f32[64,128]{1,0:T(8,128)}, f32[64,128]{1,0:T(8,128)}) custom-call(bf16[128,2048]{1,0:T(8,128)(2,1)S(1)} %bitcast.34, bf16[128,2048]{1,0:T(8,128)(2,1)S(1)} %bitcast.37, f32[168,128]{1,0:T(8,128)S(1)} %concatenate.3.pack_ref, ...), custom_call_target="tpu_custom_call" | custom-call | flops 2000000000 | bytes 6000000 | tf_op jit(solution)/shard_map/finish/pallas_call | solution.py:573
  (80 shorter events, 13.3 us)
Async XLA Ops:
  10.2 1.7 %collective-permute-start.3 = (f32[2,1,264,128]{3,2,1,0:T(8,128)S(1)}, f32[2,1,264,128]{3,2,1,0:T(8,128)S(1)}, u32[]{:S(2)}, u32[]{:S(2)}) collective-permute-start(f32[2,1,264,128]{3,2,1,0:T(8,128)S(1)} %get-tuple-element.68), channel_id=1, source_target_pairs={{0,2},{2,0},{4,6},{6,4},{8,10},{10,8},{12,14},{14,12},{16,18},{18,... | collective-permute-start | bytes 811016 | tf_op jit(solution)/shard_map/ppermute | solution.py:513
  10.7 4.2 %collective-permute-start.2 = (f32[2,1,264,128]{3,2,1,0:T(8,128)S(1)}, f32[2,1,264,128]{3,2,1,0:T(8,128)S(1)}, u32[]{:S(2)}, u32[]{:S(2)}) collective-permute-start(f32[2,1,264,128]{3,2,1,0:T(8,128)S(1)} %get-tuple-element.65), channel_id=1, source_target_pairs={{0,2},{2,0},{4,6},{6,4},{8,10},{10,8},{12,14},{14,12},{16,18},{18,... | collective-permute-start | bytes 811016 | tf_op jit(solution)/shard_map/ppermute | solution.py:513
  10.8 4.5 %collective-permute-start.1 = (f32[2,1,264,128]{3,2,1,0:T(8,128)S(1)}, f32[2,1,264,128]{3,2,1,0:T(8,128)S(1)}, u32[]{:S(2)}, u32[]{:S(2)}) collective-permute-start(f32[2,1,264,128]{3,2,1,0:T(8,128)S(1)} %get-tuple-element.62), channel_id=1, source_target_pairs={{0,2},{2,0},{4,6},{6,4},{8,10},{10,8},{12,14},{14,12},{16,18},{18,... | collective-permute-start | bytes 811016 | tf_op jit(solution)/shard_map/ppermute | solution.py:513
  11.2 5.9 %collective-permute-start = (f32[2,1,264,128]{3,2,1,0:T(8,128)S(1)}, f32[2,1,264,128]{3,2,1,0:T(8,128)S(1)}, u32[]{:S(2)}, u32[]{:S(2)}) collective-permute-start(f32[2,1,264,128]{3,2,1,0:T(8,128)S(1)} %get-tuple-element.59), channel_id=1, source_target_pairs={{0,2},{2,0},{4,6},{6,4},{8,10},{10,8},{12,14},{14,12},{16,18},{18,... | collective-permute-start | bytes 811016 | tf_op jit(solution)/shard_map/ppermute | solution.py:513
  11.9 10.6 %collective-permute-start.16 = (f32[1,264,128]{2,1,0:T(8,128)S(1)}, f32[1,264,128]{2,1,0:T(8,128)S(1)}, u32[]{:S(2)}, u32[]{:S(2)}) collective-permute-start(f32[1,264,128]{2,1,0:T(8,128)S(1)} %get-tuple-element.93), channel_id=1, source_target_pairs={{0,4},{2,6},{4,0},{6,2},{8,12},{10,14},{12,8},{14,10},{16,20},{18,... | collective-permute-start | bytes 405512 | tf_op jit(solution)/shard_map/ppermute | solution.py:513
  14.9 9.6 %collective-permute-start.12 = (f32[1,264,128]{2,1,0:T(8,128)S(1)}, f32[1,264,128]{2,1,0:T(8,128)S(1)}, u32[]{:S(2)}, u32[]{:S(2)}) collective-permute-start(f32[1,264,128]{2,1,0:T(8,128)S(1)} %get-tuple-element.87), channel_id=1, source_target_pairs={{0,4},{2,6},{4,0},{6,2},{8,12},{10,14},{12,8},{14,10},{16,20},{18,... | collective-permute-start | bytes 405512 | tf_op jit(solution)/shard_map/ppermute | solution.py:513
  15.3 9.7 %collective-permute-start.8 = (f32[1,264,128]{2,1,0:T(8,128)S(1)}, f32[1,264,128]{2,1,0:T(8,128)S(1)}, u32[]{:S(2)}, u32[]{:S(2)}) collective-permute-start(f32[1,264,128]{2,1,0:T(8,128)S(1)} %get-tuple-element.81), channel_id=1, source_target_pairs={{0,4},{2,6},{4,0},{6,2},{8,12},{10,14},{12,8},{14,10},{16,20},{18,... | collective-permute-start | bytes 405512 | tf_op jit(solution)/shard_map/ppermute | solution.py:513
  17.2 10.2 %collective-permute-start.4 = (f32[1,264,128]{2,1,0:T(8,128)S(1)}, f32[1,264,128]{2,1,0:T(8,128)S(1)}, u32[]{:S(2)}, u32[]{:S(2)}) collective-permute-start(f32[1,264,128]{2,1,0:T(8,128)S(1)} %get-tuple-element.75), channel_id=1, source_target_pairs={{0,4},{2,6},{4,0},{6,2},{8,12},{10,14},{12,8},{14,10},{16,20},{18,... | collective-permute-start | bytes 405512 | tf_op jit(solution)/shard_map/ppermute | solution.py:513
  22.6 6.8 %collective-permute-start.17 = (f32[1,264,128]{2,1,0:T(8,128)S(1)}, f32[1,264,128]{2,1,0:T(8,128)S(1)}, u32[]{:S(2)}, u32[]{:S(2)}) collective-permute-start(f32[1,264,128]{2,1,0:T(8,128)S(1)} %plane.7.refs_0_), channel_id=1, source_target_pairs={{0,8},{2,10},{4,12},{6,14},{8,0},{10,2},{12,4},{14,6},{16,24},{18,... | collective-permute-start | bytes 405512 | tf_op jit(solution)/shard_map/ppermute | solution.py:513
  24.6 7.6 %collective-permute-start.13 = (f32[1,264,128]{2,1,0:T(8,128)S(1)}, f32[1,264,128]{2,1,0:T(8,128)S(1)}, u32[]{:S(2)}, u32[]{:S(2)}) collective-permute-start(f32[1,264,128]{2,1,0:T(8,128)S(1)} %plane.6.refs_0_), channel_id=1, source_target_pairs={{0,8},{2,10},{4,12},{6,14},{8,0},{10,2},{12,4},{14,6},{16,24},{18,... | collective-permute-start | bytes 405512 | tf_op jit(solution)/shard_map/ppermute | solution.py:513
  25.0 12.8 %collective-permute-start.9 = (f32[1,264,128]{2,1,0:T(8,128)S(1)}, f32[1,264,128]{2,1,0:T(8,128)S(1)}, u32[]{:S(2)}, u32[]{:S(2)}) collective-permute-start(f32[1,264,128]{2,1,0:T(8,128)S(1)} %plane.5.refs_0_), channel_id=1, source_target_pairs={{0,8},{2,10},{4,12},{6,14},{8,0},{10,2},{12,4},{14,6},{16,24},{18,... | collective-permute-start | bytes 405512 | tf_op jit(solution)/shard_map/ppermute | solution.py:513
  27.5 12.2 %collective-permute-start.5 = (f32[1,264,128]{2,1,0:T(8,128)S(1)}, f32[1,264,128]{2,1,0:T(8,128)S(1)}, u32[]{:S(2)}, u32[]{:S(2)}) collective-permute-start(f32[1,264,128]{2,1,0:T(8,128)S(1)} %plane.4.refs_0_), channel_id=1, source_target_pairs={{0,8},{2,10},{4,12},{6,14},{8,0},{10,2},{12,4},{14,6},{16,24},{18,... | collective-permute-start | bytes 405512 | tf_op jit(solution)/shard_map/ppermute | solution.py:513
  29.4 11.7 %collective-permute-start.18 = (f32[1,128,128]{2,1,0:T(8,128)S(1)}, f32[1,128,128]{2,1,0:T(8,128)S(1)}, u32[]{:S(2)}, u32[]{:S(2)}) collective-permute-start(f32[1,128,128]{2,1,0:T(8,128)S(1)} %get-tuple-element.95), channel_id=1, source_target_pairs={{0,16},{2,18},{4,20},{6,22},{8,24},{10,26},{12,28},{14,30},{16,0},... | collective-permute-start | bytes 196616 | tf_op jit(solution)/shard_map/ppermute | solution.py:513
  32.2 10.3 %collective-permute-start.14 = (f32[1,128,128]{2,1,0:T(8,128)S(1)}, f32[1,128,128]{2,1,0:T(8,128)S(1)}, u32[]{:S(2)}, u32[]{:S(2)}) collective-permute-start(f32[1,128,128]{2,1,0:T(8,128)S(1)} %get-tuple-element.89), channel_id=1, source_target_pairs={{0,16},{2,18},{4,20},{6,22},{8,24},{10,26},{12,28},{14,30},{16,0},... | collective-permute-start | bytes 196616 | tf_op jit(solution)/shard_map/ppermute | solution.py:513
  37.9 6.5 %collective-permute-start.10 = (f32[1,128,128]{2,1,0:T(8,128)S(1)}, f32[1,128,128]{2,1,0:T(8,128)S(1)}, u32[]{:S(2)}, u32[]{:S(2)}) collective-permute-start(f32[1,128,128]{2,1,0:T(8,128)S(1)} %get-tuple-element.83), channel_id=1, source_target_pairs={{0,16},{2,18},{4,20},{6,22},{8,24},{10,26},{12,28},{14,30},{16,0},... | collective-permute-start | bytes 196616 | tf_op jit(solution)/shard_map/ppermute | solution.py:513
  39.7 6.4 %collective-permute-start.6 = (f32[1,128,128]{2,1,0:T(8,128)S(1)}, f32[1,128,128]{2,1,0:T(8,128)S(1)}, u32[]{:S(2)}, u32[]{:S(2)}) collective-permute-start(f32[1,128,128]{2,1,0:T(8,128)S(1)} %get-tuple-element.77), channel_id=1, source_target_pairs={{0,16},{2,18},{4,20},{6,22},{8,24},{10,26},{12,28},{14,30},{16,0},... | collective-permute-start | bytes 196616 | tf_op jit(solution)/shard_map/ppermute | solution.py:513
  41.1 5.7 %collective-permute-start.19 = (f32[1,256,128]{2,1,0:T(8,128)S(1)}, f32[1,256,128]{2,1,0:T(8,128)S(1)}, u32[]{:S(2)}, u32[]{:S(2)}) collective-permute-start(f32[1,256,128]{2,1,0:T(8,128)S(1)} %get-tuple-element.97), channel_id=1, source_target_pairs={{0,4},{2,6},{4,0},{6,2},{8,12},{10,14},{12,8},{14,10},{16,20},{18,... | collective-permute-start | bytes 393224 | tf_op jit(solution)/shard_map/ppermute | solution.py:513
  42.5 5.6 %collective-permute-start.15 = (f32[1,256,128]{2,1,0:T(8,128)S(1)}, f32[1,256,128]{2,1,0:T(8,128)S(1)}, u32[]{:S(2)}, u32[]{:S(2)}) collective-permute-start(f32[1,256,128]{2,1,0:T(8,128)S(1)} %get-tuple-element.91), channel_id=1, source_target_pairs={{0,4},{2,6},{4,0},{6,2},{8,12},{10,14},{12,8},{14,10},{16,20},{18,... | collective-permute-start | bytes 393224 | tf_op jit(solution)/shard_map/ppermute | solution.py:513
  44.6 6.0 %collective-permute-start.11 = (f32[1,256,128]{2,1,0:T(8,128)S(1)}, f32[1,256,128]{2,1,0:T(8,128)S(1)}, u32[]{:S(2)}, u32[]{:S(2)}) collective-permute-start(f32[1,256,128]{2,1,0:T(8,128)S(1)} %get-tuple-element.85), channel_id=1, source_target_pairs={{0,4},{2,6},{4,0},{6,2},{8,12},{10,14},{12,8},{14,10},{16,20},{18,... | collective-permute-start | bytes 393224 | tf_op jit(solution)/shard_map/ppermute | solution.py:513
  46.2 5.7 %collective-permute-start.7 = (f32[1,256,128]{2,1,0:T(8,128)S(1)}, f32[1,256,128]{2,1,0:T(8,128)S(1)}, u32[]{:S(2)}, u32[]{:S(2)}) collective-permute-start(f32[1,256,128]{2,1,0:T(8,128)S(1)} %get-tuple-element.79), channel_id=1, source_target_pairs={{0,4},{2,6},{4,0},{6,2},{8,12},{10,14},{12,8},{14,10},{16,20},{18,... | collective-permute-start | bytes 393224 | tf_op jit(solution)/shard_map/ppermute | solution.py:513
  46.9 5.2 %collective-permute-start.23 = (f32[2,1,256,128]{3,2,1,0:T(8,128)S(1)}, f32[2,1,256,128]{3,2,1,0:T(8,128)S(1)}, u32[]{:S(2)}, u32[]{:S(2)}) collective-permute-start(f32[2,1,256,128]{3,2,1,0:T(8,128)S(1)} %get-tuple-element.102), channel_id=1, source_target_pairs={{0,2},{2,0},{4,6},{6,4},{8,10},{10,8},{12,14},{14,12},{16,18},{18,... | collective-permute-start | bytes 786440 | tf_op jit(solution)/shard_map/ppermute | solution.py:513
  48.2 3.9 %collective-permute-start.22 = (f32[2,1,256,128]{3,2,1,0:T(8,128)S(1)}, f32[2,1,256,128]{3,2,1,0:T(8,128)S(1)}, u32[]{:S(2)}, u32[]{:S(2)}) collective-permute-start(f32[2,1,256,128]{3,2,1,0:T(8,128)S(1)} %get-tuple-element.101), channel_id=1, source_target_pairs={{0,2},{2,0},{4,6},{6,4},{8,10},{10,8},{12,14},{14,12},{16,18},{18,... | collective-permute-start | bytes 786440 | tf_op jit(solution)/shard_map/ppermute | solution.py:513
  50.6 1.6 %collective-permute-start.21 = (f32[2,1,256,128]{3,2,1,0:T(8,128)S(1)}, f32[2,1,256,128]{3,2,1,0:T(8,128)S(1)}, u32[]{:S(2)}, u32[]{:S(2)}) collective-permute-start(f32[2,1,256,128]{3,2,1,0:T(8,128)S(1)} %get-tuple-element.100), channel_id=1, source_target_pairs={{0,2},{2,0},{4,6},{6,4},{8,10},{10,8},{12,14},{14,12},{16,18},{18,... | collective-permute-start | bytes 786440 | tf_op jit(solution)/shard_map/ppermute | solution.py:513
  54.8 14.0 %all-to-all-start = ((f32[32,2,32]{2,1,0:T(2,128)}), f32[32,2,32]{2,1,0:T(2,128)S(1)}, u32[]{:S(2)}, u32[]{:S(2)}) async-start(f32[32,2,32]{2,1,0:T(2,128)} %broadcast_in_dim.39), calls=%async_computation | async-start | bytes 65536 | tf_op jit(solution)/shard_map/all_to_all | solution.py:572
  (11 other events, 82.4 us)

commit v3 on v2

--- a/solution.py
+++ b/solution.py
@@ -14,8 +14,9 @@
 WIDE = 256
 STATES = 64
 RESETS = 8
+MEMBERS = 1
 CHUNKS = 4
-ROOM = 16
+ROOM = 52
 NN = (((1,), (0,)), ((), ()))
 NT = (((1,), (1,)), ((), ()))
 TN = (((0,), (0,)), ((), ()))
@@ -93,9 +94,10 @@
         self.write = pack_ref[heads : heads + states].T.astype(BF16)
         self.read = pack_ref[heads + states : heads + 2 * states].T.astype(BF16)
         rows = heads + 2 * states
-        self.log_rates = pack_ref[rows : rows + 1, 0:heads]
-        self.skip = pack_ref[rows + 1 : rows + 2, 0:heads]
-        self.resets = pack_ref[rows + 2 : rows + 3].astype(jnp.int32)
+        row = pack_ref[rows : rows + 1]
+        self.log_rates = row[:, 0:heads]
+        self.skip = row[:, heads : 2 * heads]
+        self.resets = row[:, 2 * heads : 2 * heads + RESETS].astype(jnp.int32)
 
 
 def states_kernel(chunks, chips, heads, states, x_hbm, cot_hbm, pack_ref, *refs):
@@ -186,8 +188,14 @@
             put_factors(outs[shift], (part,), *both)
 
 
-def plane_kernel(chips, _, *refs):
-    gathered, out_ref = refs[:chips], refs[chips]
+def plane_kernel(chips, members, *refs):
+    out_ref = refs[members * chips]
+    parts = out_ref.shape[0] // members
+    for member in range(members):
+        plane_totals(chips, refs[member * chips : (member + 1) * chips], out_ref.at[pl.ds(member * parts, parts)])
+
+
+def plane_totals(chips, gathered, out_ref):
     _, chip, _ = position(chips)
     places = [lax.rem(chip + shift, chips) for shift in range(chips)]
     for part in range(out_ref.shape[0]):
@@ -211,9 +219,18 @@
     return lax.rem(lax.shift_right_logical(plane, level), 2)
 
 
-def hop_kernel(chips, level, last, *refs):
-    (entered_ref, refs) = (refs[0], refs[1:]) if level > 0 else (None, refs)
-    total_ref, got_ref, new_ref, onward_ref = refs
+def hop_kernel(chips, members, level, last, *refs):
+    *given, new_ref, onward_ref = refs
+    given = given[: len(given) // members * members] if members > 1 else given[: 2 + (level > 0)]
+    each = len(given) // members
+    parts = new_ref.shape[0] // members
+    for member in range(members):
+        span = pl.ds(member * parts, parts)
+        mine = given[member * each : (member + 1) * each]
+        hop_member(chips, level, last, *([None] * (3 - each)), *mine, new_ref.at[span], onward_ref.at[span])
+
+
+def hop_member(chips, level, last, entered_ref, total_ref, got_ref, new_ref, onward_ref):
     _, _, plane = position(chips)
     bit, after = half_of(plane, level), half_of(plane, level + 1)
     for part in range(got_ref.shape[0]):
@@ -240,8 +257,17 @@
             put_factors(onward_ref, (part,), *both)
 
 
-def spread_kernel(chips, level, entered_ref, got_ref, *refs):
-    gathered, outs = refs[:chips], refs[chips:]
+def spread_kernel(chips, members, level, *refs):
+    entered_ref, got_ref, *refs = refs
+    parts = got_ref.shape[0] // members
+    for member in range(members):
+        span = pl.ds(member * parts, parts)
+        gathered = refs[member * chips : (member + 1) * chips]
+        outs = refs[(members + member) * chips : (members + member + 1) * chips]
+        spread_member(chips, level, entered_ref.at[span], got_ref.at[span], gathered, outs)
+
+
+def spread_member(chips, level, entered_ref, got_ref, gathered, outs):
     _, chip, plane = position(chips)
     bit = half_of(plane, level)
     places = [lax.rem(chip + shift, chips) for shift in range(chips)]
@@ -273,7 +299,8 @@
                 outs[target][part, rows_of(scan)] = total
 
 
-def core_kernel(chips, keep_ref, got_ref, *refs):
+def core_kernel(chips, extra, *refs):
+    keep_ref, got_ref, *refs = refs[extra:]
     entered, (own_ref, send_ref) = refs[:chips], refs[chips:]
     core, chip, _ = position(chips)
     for shift in range(chips):
@@ -315,7 +342,7 @@
 
 
 def inner_kernel(heads, states, x_ref, cot_ref, pack_ref, *outs):
-    y_ref, g_ref, flow_ref, gread_ref, gwrite_ref, rate_ref = outs[-6:]
+    flow_ref, gread_ref, gwrite_ref, rate_ref = outs[-4:]
     length, channels = x_ref.shape
     given = Packed(pack_ref, heads, states)
     deltas, own = given.deltas, Block(given)
@@ -341,8 +368,6 @@
         y_f, y_r = u_f * pre_f, u_r * pre_r
         g_f, g_r = v_f * mm(scores_f, ct_f, TN), v_r * mm(scores_r, ct_r, TN)
         grad = g_f + g_r
-        y_ref[:, lanes] = (y_f + y_r).astype(BF16)
-        g_ref[:, lanes] = grad.astype(BF16)
         flow = flow + reduced(jnp.concatenate([cot * y_f - scaled * g_f, cot * y_r - scaled * g_r, x * grad], axis=0), expand[:heads])
         pair_f = pair_f + mm(ct_f, sc_f, NT)
         pair_r = pair_r + mm(ct_r, sc_r, NT)
@@ -392,12 +417,15 @@
 
 
 def finish_kernel(chunks, chips, heads, states, x_ref, cot_ref, pack_ref, *refs):
-    y_ref, g_ref, flow_ref, gread0_ref, gwrite0_ref = refs[:5]
-    entered, got = refs[5 : 5 + chunks], refs[5 + chunks : 5 + 2 * chunks]
-    out_ref, gin_ref, steps_ref, gwrite_ref, gread_ref = refs[5 + 2 * chunks :]
+    flow_ref, gread0_ref, gwrite0_ref = refs[:3]
+    entered, got = refs[3 : 3 + chunks], refs[3 + chunks : 3 + 2 * chunks]
+    out_ref, gin_ref, steps_ref, gwrite_ref, gread_ref = refs[3 + 2 * chunks :]
     length, channels = x_ref.shape
     given = Packed(pack_ref, heads, states)
     deltas, own = given.deltas, Block(given)
+    scores = mm(own.read, own.write, NT)
+    scores_f = jnp.where(own.mask_f, scores, 0.0).astype(BF16)
+    scores_r = jnp.where(own.mask_r, scores, 0.0).astype(BF16)
     skip = jnp.broadcast_to(given.skip, (8, heads))
     parts = spread_parts(factors(deltas, own.lam, own.cum) + [skip])
     flow = flow_ref[...]
@@ -423,9 +451,11 @@
         back_f16, back_r16 = (back_f * chain).astype(BF16), back_r.astype(BF16)
         y_f, y_r = u_f * mm(own.read_f, in_f16), u_r * mm(own.read_r, in_r16)
         g_f, g_r = v_f * mm(own.write_f, back_f16), v_r * mm(own.write_r, back_r16)
-        out_ref[:, lanes] = (y_ref[:, lanes] + (y_f + y_r) + gain * x).astype(BF16)
+        inside = u_f * mm(scores_f, sc_f) + u_r * mm(scores_r, sc_r)
+        inside_grad = v_f * mm(scores_f, ct_f, TN) + v_r * mm(scores_r, ct_r, TN)
+        out_ref[:, lanes] = (inside + (y_f + y_r) + gain * x).astype(BF16)
         grad = g_f + g_r
-        gin_ref[:, lanes] = (step * (g_ref[:, lanes] + grad) + gain * cot).astype(BF16)
+        gin_ref[:, lanes] = (step * (inside_grad + grad) + gain * cot).astype(BF16)
         local_f, local_r = mm(own.write_f, sc_f, TN) * chain, mm(own.write_r, sc_r, TN)
         through = back_f * (local_f + own.open_f * chain * in_f) + back_r * (local_r + own.open_r * chain * in_r)
         through = jnp.sum(through, axis=0, keepdims=True)
@@ -468,8 +498,8 @@
     levels = int(math.log2(planes))
     chunks = min(CHUNKS, channels // (WIDE * chips))
     parts = channels // (WIDE * chips * chunks)
-    lined = [jnp.pad(row.astype(F32)[None], ((0, 0), (0, length - row.shape[0]))) for row in (log_rates, skip_gain, resets[0])]
-    pack = jnp.concatenate([deltas, write.astype(F32), read.astype(F32), *lined, jnp.zeros((5, length), F32)], axis=0)
+    line = jnp.concatenate([log_rates, skip_gain, resets[0].astype(F32), jnp.zeros((length - 2 * heads - RESETS,), F32)])
+    pack = jnp.concatenate([deltas, write.astype(F32), read.astype(F32), jnp.broadcast_to(line[None], (8, length))], axis=0)
 
     def like(*shape, kind=F32):
         return jax.ShapeDtypeStruct(shape, kind)
@@ -516,11 +546,54 @@
     for k in range(chunks):
         gots.append(send_to(send[k], swap))
         chipped.append(call(functools.partial(chip_kernel, chips), [single] * chips, [vmem] * 2, 10**6, 10**6, "chip")(keep[k], gots[k]))
+    size = 4 * parts * states * LANES * 4
+    gathered = []
+    for k in range(chunks):
+        pieces = [chipped[k][0]] + [None] * (chips - 1)
+        for shift in range(1, chips):
+            pieces[chips - shift] = send_to(chipped[k][shift], turn(shift))
+        gathered.append(pieces)
+    extra, arrivals, far_states = 1, [], []
+    members = math.gcd(MEMBERS, chunks)
+    merged = like(members * parts, message, LANES)
+    merged_half = like(members * parts, 2 * states, LANES)
+    owns, theirs_in = [], []
+    for group_start in range(0, chunks, members):
+        chunk_range = range(group_start, group_start + members)
+        pieces = [piece for k in chunk_range for piece in gathered[k]]
+        given = []
+        for k in chunk_range:
+            onward = call(functools.partial(plane_kernel, chips, 1), single, [vmem] * chips, 10**6, size * 3, "plane")(
+                *gathered[k]
+            )
+            before = []
+            for level in range(levels - 2):
+                arrived = send_to(onward, across(level))
+                step = functools.partial(hop_kernel, chips, 1, level, False)
+                entry, onward = call(step, [single] * 2, [vmem] * (2 + len(before)), 10**6, size * 4, "hop")(*before, onward, arrived)
+                before = [entry]
+            given += [*before, onward, send_to(onward, across(levels - 2))]
+        step = functools.partial(hop_kernel, chips, members, levels - 2, True)
+        behind = arrivals[-2][:1] if len(arrivals) >= 2 else []
+        spaces = [vmem] * len(given) + [pl.ANY] * len(behind)
+        entry, onward = call(step, [merged, merged_half], spaces, 10**6, size * 4, "hop")(*given, *behind)
+        before = [entry]
+        arrived = send_to(onward, across(levels - 1))
+        placed = call(
+            functools.partial(spread_kernel, chips, members, levels - 1),
+            [bare] * (chips * members),
+            [vmem] * (2 + chips * members),
+            10**6,
+            size * 5,
+            "spread",
+        )(*before, arrived, *pieces)
+        for member in range(members):
+            mine = placed[member * chips : (member + 1) * chips]
+            arrivals.append(mine)
+            far_states.append([send_to(mine[shift], turn(shift)) for shift in range(1, chips)])
     inner = call(
         functools.partial(inner_kernel, heads, states),
         [
-            like(length, channels, kind=BF16),
-            like(length, channels, kind=BF16),
             like(3 * length, heads),
             like(length, states),
             like(length, states),
@@ -530,43 +603,17 @@
         10**9,
         8 * 10**6,
         "inner",
-    )(x, cot, pack, *[value[0] for value in chipped])
-    size = 4 * parts * states * LANES * 4
-    owns, theirs_in = [], []
+    )(x, cot, pack, *[value[0] for value in arrivals])
     for k in range(chunks):
-        got, chip_totals = gots[k], chipped[k]
-        gathered = [chip_totals[0]] + [None] * (chips - 1)
-        for shift in range(1, chips):
-            gathered[chips - shift] = send_to(chip_totals[shift], turn(shift))
-        onward = call(functools.partial(plane_kernel, chips), single, [pl.ANY] + [vmem] * chips, 10**6, size * 3, "plane")(inner[3], *gathered)
-        before = []
-        for level in range(levels - 1):
-            arrived = send_to(onward, across(level))
-            last = level == levels - 2
-            hop = call(
-                functools.partial(hop_kernel, chips, level, last),
-                [single, half if last else single],
-                [vmem] * (2 + len(before)),
-                10**6,
-                size * 4,
-                "hop",
-            )
-            entry, onward = hop(*before, onward, arrived)
-            before = [entry]
-        arrived = send_to(onward, across(levels - 1))
-        placed = call(
-            functools.partial(spread_kernel, chips, levels - 1), [bare] * chips, [vmem] * (2 + chips), 10**6, size * 5, "spread"
-        )(*before, arrived, *gathered)
-        entered = [placed[0]] + [send_to(placed[shift], turn(shift)) for shift in range(1, chips)]
-        mine, theirs = call(functools.partial(core_kernel, chips), [pair] * 2, [vmem] * (2 + chips), 10**6, size * 8, "core")(
-            keep[k], got, *entered
-        )
+        mine, theirs = call(
+            functools.partial(core_kernel, chips, extra), [pair] * 2, [pl.ANY] + [vmem] * (2 + chips), 10**6, size * 8, "core"
+        )(inner[1], keep[k], gots[k], arrivals[k][0], *far_states[k])
         owns.append(mine)
         theirs_in.append(send_to(theirs, swap))
 
     small = call(
         functools.partial(rates_kernel, chunks, chips), like(2, heads), [vmem] * (1 + 2 * chunks), 10**6, 4 * 10**6, "rates"
-    )(inner[5], *owns, *theirs_in)
+    )(inner[3], *owns, *theirs_in)
     count = devices * lax.axis_size("dp")
     copies = jnp.broadcast_to(small[None], (count,) + small.shape)
     total = jnp.sum(lax.all_to_all(copies, ("seq", "dp"), 0, 0, tiled=True), axis=0)
@@ -579,11 +626,11 @@
             like(states, length),
             like(states, length),
         ],
-        [vmem] * (8 + 2 * chunks),
+        [vmem] * (6 + 2 * chunks),
         2 * 10**9,
         6 * 10**6,
         "finish",
-    )(x, cot, pack, *inner[:5], *owns, *theirs_in)
+    )(x, cot, pack, *inner[:3], *owns, *theirs_in)
     return (outputs[None], grad_inputs[None], grad_steps.T[None], grad_write.T[None], grad_read.T[None], total[0], total[1])
 
 

time: 69.9 us -> 66.1 us (0.946)
  local copies, waits for them, and re-layouts: 8.25 us -> 2.01 us
  Pallas kernels: 16.1 us -> 17.6 us
  other arithmetic: 1.44 us -> 2.92 us
  starting transfers between devices: 31.7 us -> 30.7 us
    unnamed x20 -> x8, local copies, waits for them, and re-layouts: 5.02 us -> 0.85 us
    all_to_all x1, starting transfers between devices: 5.49 us -> 3.07 us  [local(): lax.all_to_all(copies, ('seq', 'dp'), 0, 0, tiled=True)]
    concatenate x0 -> x2, other arithmetic: none -> 1.47 us  [the longest x1 0.75 us: local(): jnp.concatenate([log_rates, skip_gain, resets[0].astype(F32), jnp.zeros((...]
    ppermute x24, starting transfers between devices: 26.2 us -> 27.7 us  [send_to(): return lax.ppermute(value, 'seq', perm)]
    pad x3 -> x0, local copies, waits for them, and re-layouts: 1.33 us -> none  [local(): jnp.pad(row.astype(F32)[None], ((0, 0), (0, length - row.shape[0])))]
    pallas_call x1, Pallas kernels: 3.98 us -> 5.1 us  [local(): call(functools.partial(states_kernel, chunks, chips, heads, states), [gro...]
    concatenate x1 -> x0, local copies, waits for them, and re-layouts: 0.74 us -> none  [local(): jnp.concatenate([deltas, write.astype(F32), read.astype(F32), *lined, jnp...]
  transfers between devices with their start and end apart: 25 -> 25, of which waited for: 11 -> 13; matrix products, arithmetic and copies ran while one was open for 0% -> 0% of each run, Pallas kernels for 17% -> 18%
where the time goes in v3:
time: 66.1 us; the launch traced here: 65.6 us
  starting transfers between devices  30.7 us (46%)
  Pallas kernels  17.6 us (27%)
  waiting for transfers between devices  11.5 us (17%)
  other arithmetic  2.92 us (4%)
  local copies, waits for them, and re-layouts  2.01 us (3%)
  between operations  0.83 us (1%)
    ppermute x24, starting transfers between devices, send_to(): return lax.ppermute(value, 'seq', perm)  27.7 us
    ppermute x24, waiting for transfers between devices, send_to(): return lax.ppermute(value, 'seq', perm)  11.1 us
    pallas_call x1, Pallas kernels, local(): call(functools.partial(finish_kernel, chunks, chips, heads, states), [lik...  5.96 us
    pallas_call x1, Pallas kernels, local(): call(functools.partial(states_kernel, chunks, chips, heads, states), [gro...  5.1 us
    pallas_call x1, Pallas kernels, local(): call(functools.partial(inner_kernel, heads, states), [like(3 * length, he...  4.93 us
    all_to_all x1, starting transfers between devices, local(): lax.all_to_all(copies, ('seq', 'dp'), 0, 0, tiled=True)  3.07 us
  transfers between devices with their start and end apart: 25, of which 13 were waited for; matrix products, arithmetic and copies ran while one was open for 0% of the time, Pallas kernels for 18%

profile of v3, /device:TPU:0, one launch (start us, length us, event | category | flops | bytes accessed | tf_op | source)
XLA Modules:
  0.0 65.6 jit_solution(9826992308482172460)
XLA Ops:
  0.6 0.7 %convert_bitcast_fusion.2 = f32[8]{0:T(128)S(1)} fusion(s32[1,8]{1,0:T(1,128)} %param.14), kind=kLoop, calls=%fused_computation.6 | loop fusion | flops 8 | bytes 64 | tf_op jit(solution)/shard_map/convert_element_type | solution.py:501
  1.3 0.7 %convert_bitcast_fusion = (f32[64,128]{1,0:T(8,128)S(1)}, f32[64,128]{1,0:T(8,128)S(1)}) fusion(bf16[1,128,64]{1,2,0:T(8,128)(2,1)} %param.11, bf16[1,128,64]{1,2,0:T(8,128)(2,1)} %param.10), kind=kLoop, calls=%fused_computation.1 | loop fusion | flops 16384 | bytes 98304 | tf_op jit(solution)/shard_map/convert_element_type | solution.py:502
  2.0 0.7 %pad_maximum_fusion.1 = f32[128]{0:T(128)S(1)} fusion(f32[56]{0:T(128)S(1)} %broadcast_in_dim.30, f32[8]{0:T(128)S(1)} %convert_bitcast_fusion.2, f32[32]{0:T(128)} %param.13, f32[32]{0:T(128)} %param.12), kind=kLoop, calls=%fused_computation.3 | loop fusion | flops 384 | bytes 1024 | tf_op jit(solution)/shard_map/concatenate | solution.py:501
  2.8 0.7 %pad_maximum_fusion.pack_ref = f32[168,128]{1,0:T(8,128)S(1)} fusion(f32[8,128]{1,0:T(8,128)S(1)} %broadcast_in_dim.31, f32[64,128]{1,0:T(8,128)S(1)} %get-tuple-element.107, f32[64,128]{1,0:T(8,128)S(1)} %get-tuple-element.108, f32[32,128]{1,0:T(8,128)} %bitcast.38), kind=kLoop, calls=%fused_computation | loop fusion | flops 64512 | bytes 172032 | tf_op jit(solution)/shard_map/concatenate | solution.py:502
  3.5 5.1 %states.1 = (f32[2,1,264,128]{3,2,1,0:T(8,128)S(1)}, f32[2,1,264,128]{3,2,1,0:T(8,128)S(1)}, f32[2,1,264,128]{3,2,1,0:T(8,128)S(1)}, f32[2,1,264,128]{3,2,1,0:T(...) custom-call(bf16[128,2048]{1,0:T(8,128)(2,1)} %bitcast.32, ...), custom_call_target="tpu_custom_call" | custom-call | flops 300000000 | bytes 4000000 | tf_op jit(solution)/shard_map/states/pallas_call | solution.py:514
  10.4 2.9 %collective-permute-start.5 = (f32[1,264,128]{2,1,0:T(8,128)S(1)}, f32[1,264,128]{2,1,0:T(8,128)S(1)}, u32[]{:S(2)}, u32[]{:S(2)}) collective-permute-start(f32[1,264,128]{2,1,0:T(8,128)S(1)} %get-tuple-element.66), channel_id=1, source_target_pairs={{0,4},{2,6},{4,0},{6,2},{8,12},{10,14},{12,8},{14,10},{16,20},{18,... | collective-permute-start | bytes 405512 | tf_op jit(solution)/shard_map/ppermute | solution.py:543
  13.7 1.8 %collective-permute-start.13 = (f32[1,264,128]{2,1,0:T(8,128)S(1)}, f32[1,264,128]{2,1,0:T(8,128)S(1)}, u32[]{:S(2)}, u32[]{:S(2)}) collective-permute-start(f32[1,264,128]{2,1,0:T(8,128)S(1)} %get-tuple-element.80), channel_id=1, source_target_pairs={{0,4},{2,6},{4,0},{6,2},{8,12},{10,14},{12,8},{14,10},{16,20},{18,... | collective-permute-start | bytes 405512 | tf_op jit(solution)/shard_map/ppermute | solution.py:543
  16.0 1.7 %collective-permute-done.5.refs_1_.refs_3_ = f32[1,264,128]{2,1,0:T(8,128)S(1)} collective-permute-done((f32[1,264,128]{2,1,0:T(8,128)S(1)}, f32[1,264,128]{2,1,0:T(8,128)S(1)}, u32[]{:S(2)}, u32[]{:S(2)}) %collective-permute-start.5) | collective-permute-done | bytes 135200 | tf_op jit(solution)/shard_map/ppermute | solution.py:543
  17.7 2.2 %collective-permute-start.6 = (f32[1,264,128]{2,1,0:T(8,128)S(1)}, f32[1,264,128]{2,1,0:T(8,128)S(1)}, u32[]{:S(2)}, u32[]{:S(2)}) collective-permute-start(f32[1,264,128]{2,1,0:T(8,128)S(1)} %plane.5.refs_0_), channel_id=1, source_target_pairs={{0,8},{2,10},{4,12},{6,14},{8,0},{10,2},{12,4},{14,6},{16,24},{18,... | collective-permute-start | bytes 405512 | tf_op jit(solution)/shard_map/ppermute | solution.py:543
  20.6 2.2 %collective-permute-start.2 = (f32[1,264,128]{2,1,0:T(8,128)S(1)}, f32[1,264,128]{2,1,0:T(8,128)S(1)}, u32[]{:S(2)}, u32[]{:S(2)}) collective-permute-start(f32[1,264,128]{2,1,0:T(8,128)S(1)} %plane.4.refs_0_), channel_id=1, source_target_pairs={{0,8},{2,10},{4,12},{6,14},{8,0},{10,2},{12,4},{14,6},{16,24},{18,... | collective-permute-start | bytes 405512 | tf_op jit(solution)/shard_map/ppermute | solution.py:543
  23.5 2.2 %collective-permute-start.14 = (f32[1,264,128]{2,1,0:T(8,128)S(1)}, f32[1,264,128]{2,1,0:T(8,128)S(1)}, u32[]{:S(2)}, u32[]{:S(2)}) collective-permute-start(f32[1,264,128]{2,1,0:T(8,128)S(1)} %plane.7.refs_0_), channel_id=1, source_target_pairs={{0,8},{2,10},{4,12},{6,14},{8,0},{10,2},{12,4},{14,6},{16,24},{18,... | collective-permute-start | bytes 405512 | tf_op jit(solution)/shard_map/ppermute | solution.py:543
  25.9 1.9 %collective-permute-start.10 = (f32[1,264,128]{2,1,0:T(8,128)S(1)}, f32[1,264,128]{2,1,0:T(8,128)S(1)}, u32[]{:S(2)}, u32[]{:S(2)}) collective-permute-start(f32[1,264,128]{2,1,0:T(8,128)S(1)} %plane.6.refs_0_), channel_id=1, source_target_pairs={{0,8},{2,10},{4,12},{6,14},{8,0},{10,2},{12,4},{14,6},{16,24},{18,... | collective-permute-start | bytes 405512 | tf_op jit(solution)/shard_map/ppermute | solution.py:543
  27.8 2.7 %collective-permute-start.7 = (f32[1,128,128]{2,1,0:T(8,128)S(1)}, f32[1,128,128]{2,1,0:T(8,128)S(1)}, u32[]{:S(2)}, u32[]{:S(2)}) collective-permute-start(f32[1,128,128]{2,1,0:T(8,128)S(1)} %get-tuple-element.68), channel_id=1, source_target_pairs={{0,16},{2,18},{4,20},{6,22},{8,24},{10,26},{12,28},{14,30},{16,0},... | collective-permute-start | bytes 196616 | tf_op jit(solution)/shard_map/ppermute | solution.py:543
  30.9 2.8 %collective-permute-done.7.refs_1_ = f32[1,128,128]{2,1,0:T(8,128)S(1)} collective-permute-done((f32[1,128,128]{2,1,0:T(8,128)S(1)}, f32[1,128,128]{2,1,0:T(8,128)S(1)}, u32[]{:S(2)}, u32[]{:S(2)}) %collective-permute-start.7) | collective-permute-done | bytes 65568 | tf_op jit(solution)/shard_map/ppermute | solution.py:543
  33.9 3.0 %collective-permute-start.15 = (f32[1,128,128]{2,1,0:T(8,128)S(1)}, f32[1,128,128]{2,1,0:T(8,128)S(1)}, u32[]{:S(2)}, u32[]{:S(2)}) collective-permute-start(f32[1,128,128]{2,1,0:T(8,128)S(1)} %get-tuple-element.82), channel_id=1, source_target_pairs={{0,16},{2,18},{4,20},{6,22},{8,24},{10,26},{12,28},{14,30},{16,0},... | collective-permute-start | bytes 196616 | tf_op jit(solution)/shard_map/ppermute | solution.py:543
  36.9 1.9 %collective-permute-done.3.refs_1_ = f32[1,128,128]{2,1,0:T(8,128)S(1)} collective-permute-done((f32[1,128,128]{2,1,0:T(8,128)S(1)}, f32[1,128,128]{2,1,0:T(8,128)S(1)}, u32[]{:S(2)}, u32[]{:S(2)}) %collective-permute-start.3) | collective-permute-done | bytes 65568 | tf_op jit(solution)/shard_map/ppermute | solution.py:543
  39.0 1.6 %collective-permute-start.17 = (f32[1,256,128]{2,1,0:T(8,128)S(1)}, f32[1,256,128]{2,1,0:T(8,128)S(1)}, u32[]{:S(2)}, u32[]{:S(2)}) collective-permute-start(f32[1,256,128]{2,1,0:T(8,128)S(1)} %get-tuple-element.89), channel_id=1, source_target_pairs={{0,4},{2,6},{4,0},{6,2},{8,12},{10,14},{12,8},{14,10},{16,20},{18,... | collective-permute-start | bytes 393224 | tf_op jit(solution)/shard_map/ppermute | solution.py:543
  41.1 1.6 %collective-permute-start.19 = (f32[1,256,128]{2,1,0:T(8,128)S(1)}, f32[1,256,128]{2,1,0:T(8,128)S(1)}, u32[]{:S(2)}, u32[]{:S(2)}) collective-permute-start(f32[1,256,128]{2,1,0:T(8,128)S(1)} %get-tuple-element.93), channel_id=1, source_target_pairs={{0,4},{2,6},{4,0},{6,2},{8,12},{10,14},{12,8},{14,10},{16,20},{18,... | collective-permute-start | bytes 393224 | tf_op jit(solution)/shard_map/ppermute | solution.py:543
  42.7 1.4 %collective-permute-done.11.refs_1_ = f32[1,128,128]{2,1,0:T(8,128)S(1)} collective-permute-done((f32[1,128,128]{2,1,0:T(8,128)S(1)}, f32[1,128,128]{2,1,0:T(8,128)S(1)}, u32[]{:S(2)}, u32[]{:S(2)}) %collective-permute-start.11) | collective-permute-done | bytes 65568 | tf_op jit(solution)/shard_map/ppermute | solution.py:543
  44.2 1.6 %collective-permute-start.18 = (f32[1,256,128]{2,1,0:T(8,128)S(1)}, f32[1,256,128]{2,1,0:T(8,128)S(1)}, u32[]{:S(2)}, u32[]{:S(2)}) collective-permute-start(f32[1,256,128]{2,1,0:T(8,128)S(1)} %get-tuple-element.91), channel_id=1, source_target_pairs={{0,4},{2,6},{4,0},{6,2},{8,12},{10,14},{12,8},{14,10},{16,20},{18,... | collective-permute-start | bytes 393224 | tf_op jit(solution)/shard_map/ppermute | solution.py:543
  45.8 4.9 %inner.1 = (f32[384,32]{1,0:T(8,128)S(1)}, f32[128,64]{1,0:T(8,128)S(1)}, f32[128,64]{1,0:T(8,128)S(1)}, f32[8,264,256]{2,1,0:T(8,128)S(1)}) custom-call(bf16[128,2048]{1,0:T(8,128)(2,1)S(1)} %bitcast.33, bf16[128,2048]{1,0:T(8,128)(2,1)S(1)} %bitcast.36, f32[168,128]{1,0:T(8,128)S(1)} %pad_maximum_fusion.pack_ref, ...), custom_call_target="tpu_custom_call" | custom-call | flops 1000000000 | bytes 8000000 | tf_op jit(solution)/shard_map/inner/pallas_call | solution.py:594
  54.8 3.1 %all-to-all-start = ((f32[32,2,32]{2,1,0:T(2,128)}), f32[32,2,32]{2,1,0:T(2,128)S(1)}, u32[]{:S(2)}, u32[]{:S(2)}) async-start(f32[32,2,32]{2,1,0:T(2,128)} %broadcast_in_dim.37), calls=%async_computation | async-start | bytes 65536 | tf_op jit(solution)/shard_map/all_to_all | solution.py:619
  57.9 0.8 %copy-done.3 = f32[128,64]{1,0:T(8,128)S(1)} copy-done((f32[128,64]{1,0:T(8,128)S(1)}, f32[128,64]{1,0:T(8,128)}, u32[]{:S(2)}) %copy-start.3) | copy-done | bytes 32792
  58.7 6.0 %finish.1 = (bf16[128,2048]{1,0:T(8,128)(2,1)}, bf16[128,2048]{1,0:T(8,128)(2,1)}, f32[32,128]{1,0:T(8,128)}, f32[64,128]{1,0:T(8,128)}, f32[64,128]{1,0:T(8,128)}) custom-call(bf16[128,2048]{1,0:T(8,128)(2,1)S(1)} %bitcast.34, bf16[128,2048]{1,0:T(8,128)(2,1)S(1)} %bitcast.37, f32[168,128]{1,0:T(8,128)S(1)} %pad_maximum_fusion.pack_ref, ...), custom_call_target="tpu_custom_call" | custom-call | flops 2000000000 | bytes 6000000 | tf_op jit(solution)/shard_map/finish/pallas_call | solution.py:620
  (67 shorter events, 10.6 us)
Async XLA Ops:
  8.6 1.7 %collective-permute-start.4 = (f32[2,1,264,128]{3,2,1,0:T(8,128)S(1)}, f32[2,1,264,128]{3,2,1,0:T(8,128)S(1)}, u32[]{:S(2)}, u32[]{:S(2)}) collective-permute-start(f32[2,1,264,128]{3,2,1,0:T(8,128)S(1)} %get-tuple-element.64), channel_id=1, source_target_pairs={{0,2},{2,0},{4,6},{6,4},{8,10},{10,8},{12,14},{14,12},{16,18},{18,... | collective-permute-start | bytes 811016 | tf_op jit(solution)/shard_map/ppermute | solution.py:543
  9.1 4.2 %collective-permute-start = (f32[2,1,264,128]{3,2,1,0:T(8,128)S(1)}, f32[2,1,264,128]{3,2,1,0:T(8,128)S(1)}, u32[]{:S(2)}, u32[]{:S(2)}) collective-permute-start(f32[2,1,264,128]{3,2,1,0:T(8,128)S(1)} %get-tuple-element.57), channel_id=1, source_target_pairs={{0,2},{2,0},{4,6},{6,4},{8,10},{10,8},{12,14},{14,12},{16,18},{18,... | collective-permute-start | bytes 811016 | tf_op jit(solution)/shard_map/ppermute | solution.py:543
  9.2 4.5 %collective-permute-start.12 = (f32[2,1,264,128]{3,2,1,0:T(8,128)}, f32[2,1,264,128]{3,2,1,0:T(8,128)S(1)}, u32[]{:S(2)}, u32[]{:S(2)}) collective-permute-start(f32[2,1,264,128]{3,2,1,0:T(8,128)} %get-tuple-element.78), channel_id=1, source_target_pairs={{0,2},{2,0},{4,6},{6,4},{8,10},{10,8},{12,14},{14,12},{16,18},{18,... | collective-permute-start | bytes 811016 | tf_op jit(solution)/shard_map/ppermute | solution.py:543
  9.6 5.9 %collective-permute-start.8 = (f32[2,1,264,128]{3,2,1,0:T(8,128)S(1)}, f32[2,1,264,128]{3,2,1,0:T(8,128)S(1)}, u32[]{:S(2)}, u32[]{:S(2)}) collective-permute-start(f32[2,1,264,128]{3,2,1,0:T(8,128)S(1)} %get-tuple-element.71), channel_id=1, source_target_pairs={{0,2},{2,0},{4,6},{6,4},{8,10},{10,8},{12,14},{14,12},{16,18},{18,... | collective-permute-start | bytes 811016 | tf_op jit(solution)/shard_map/ppermute | solution.py:543
  10.4 7.3 %collective-permute-start.5 = (f32[1,264,128]{2,1,0:T(8,128)S(1)}, f32[1,264,128]{2,1,0:T(8,128)S(1)}, u32[]{:S(2)}, u32[]{:S(2)}) collective-permute-start(f32[1,264,128]{2,1,0:T(8,128)S(1)} %get-tuple-element.66), channel_id=1, source_target_pairs={{0,4},{2,6},{4,0},{6,2},{8,12},{10,14},{12,8},{14,10},{16,20},{18,... | collective-permute-start | bytes 405512 | tf_op jit(solution)/shard_map/ppermute | solution.py:543
  13.4 7.2 %collective-permute-start.1 = (f32[1,264,128]{2,1,0:T(8,128)S(1)}, f32[1,264,128]{2,1,0:T(8,128)S(1)}, u32[]{:S(2)}, u32[]{:S(2)}) collective-permute-start(f32[1,264,128]{2,1,0:T(8,128)S(1)} %get-tuple-element.59), channel_id=1, source_target_pairs={{0,4},{2,6},{4,0},{6,2},{8,12},{10,14},{12,8},{14,10},{16,20},{18,... | collective-permute-start | bytes 405512 | tf_op jit(solution)/shard_map/ppermute | solution.py:543
  13.7 9.7 %collective-permute-start.13 = (f32[1,264,128]{2,1,0:T(8,128)S(1)}, f32[1,264,128]{2,1,0:T(8,128)S(1)}, u32[]{:S(2)}, u32[]{:S(2)}) collective-permute-start(f32[1,264,128]{2,1,0:T(8,128)S(1)} %get-tuple-element.80), channel_id=1, source_target_pairs={{0,4},{2,6},{4,0},{6,2},{8,12},{10,14},{12,8},{14,10},{16,20},{18,... | collective-permute-start | bytes 405512 | tf_op jit(solution)/shard_map/ppermute | solution.py:543
  15.6 10.2 %collective-permute-start.9 = (f32[1,264,128]{2,1,0:T(8,128)S(1)}, f32[1,264,128]{2,1,0:T(8,128)S(1)}, u32[]{:S(2)}, u32[]{:S(2)}) collective-permute-start(f32[1,264,128]{2,1,0:T(8,128)S(1)} %get-tuple-element.73), channel_id=1, source_target_pairs={{0,4},{2,6},{4,0},{6,2},{8,12},{10,14},{12,8},{14,10},{16,20},{18,... | collective-permute-start | bytes 405512 | tf_op jit(solution)/shard_map/ppermute | solution.py:543
  17.7 10.1 %collective-permute-start.6 = (f32[1,264,128]{2,1,0:T(8,128)S(1)}, f32[1,264,128]{2,1,0:T(8,128)S(1)}, u32[]{:S(2)}, u32[]{:S(2)}) collective-permute-start(f32[1,264,128]{2,1,0:T(8,128)S(1)} %plane.5.refs_0_), channel_id=1, source_target_pairs={{0,8},{2,10},{4,12},{6,14},{8,0},{10,2},{12,4},{14,6},{16,24},{18,... | collective-permute-start | bytes 405512 | tf_op jit(solution)/shard_map/ppermute | solution.py:543
  20.6 9.9 %collective-permute-start.2 = (f32[1,264,128]{2,1,0:T(8,128)S(1)}, f32[1,264,128]{2,1,0:T(8,128)S(1)}, u32[]{:S(2)}, u32[]{:S(2)}) collective-permute-start(f32[1,264,128]{2,1,0:T(8,128)S(1)} %plane.4.refs_0_), channel_id=1, source_target_pairs={{0,8},{2,10},{4,12},{6,14},{8,0},{10,2},{12,4},{14,6},{16,24},{18,... | collective-permute-start | bytes 405512 | tf_op jit(solution)/shard_map/ppermute | solution.py:543
  23.5 10.3 %collective-permute-start.14 = (f32[1,264,128]{2,1,0:T(8,128)S(1)}, f32[1,264,128]{2,1,0:T(8,128)S(1)}, u32[]{:S(2)}, u32[]{:S(2)}) collective-permute-start(f32[1,264,128]{2,1,0:T(8,128)S(1)} %plane.7.refs_0_), channel_id=1, source_target_pairs={{0,8},{2,10},{4,12},{6,14},{8,0},{10,2},{12,4},{14,6},{16,24},{18,... | collective-permute-start | bytes 405512 | tf_op jit(solution)/shard_map/ppermute | solution.py:543
  25.9 12.9 %collective-permute-start.10 = (f32[1,264,128]{2,1,0:T(8,128)S(1)}, f32[1,264,128]{2,1,0:T(8,128)S(1)}, u32[]{:S(2)}, u32[]{:S(2)}) collective-permute-start(f32[1,264,128]{2,1,0:T(8,128)S(1)} %plane.6.refs_0_), channel_id=1, source_target_pairs={{0,8},{2,10},{4,12},{6,14},{8,0},{10,2},{12,4},{14,6},{16,24},{18,... | collective-permute-start | bytes 405512 | tf_op jit(solution)/shard_map/ppermute | solution.py:543
  27.8 5.9 %collective-permute-start.7 = (f32[1,128,128]{2,1,0:T(8,128)S(1)}, f32[1,128,128]{2,1,0:T(8,128)S(1)}, u32[]{:S(2)}, u32[]{:S(2)}) collective-permute-start(f32[1,128,128]{2,1,0:T(8,128)S(1)} %get-tuple-element.68), channel_id=1, source_target_pairs={{0,16},{2,18},{4,20},{6,22},{8,24},{10,26},{12,28},{14,30},{16,0},... | collective-permute-start | bytes 196616 | tf_op jit(solution)/shard_map/ppermute | solution.py:543
  30.5 8.2 %collective-permute-start.3 = (f32[1,128,128]{2,1,0:T(8,128)S(1)}, f32[1,128,128]{2,1,0:T(8,128)S(1)}, u32[]{:S(2)}, u32[]{:S(2)}) collective-permute-start(f32[1,128,128]{2,1,0:T(8,128)S(1)} %get-tuple-element.61), channel_id=1, source_target_pairs={{0,16},{2,18},{4,20},{6,22},{8,24},{10,26},{12,28},{14,30},{16,0},... | collective-permute-start | bytes 196616 | tf_op jit(solution)/shard_map/ppermute | solution.py:543
  33.9 7.2 %collective-permute-start.15 = (f32[1,128,128]{2,1,0:T(8,128)S(1)}, f32[1,128,128]{2,1,0:T(8,128)S(1)}, u32[]{:S(2)}, u32[]{:S(2)}) collective-permute-start(f32[1,128,128]{2,1,0:T(8,128)S(1)} %get-tuple-element.82), channel_id=1, source_target_pairs={{0,16},{2,18},{4,20},{6,22},{8,24},{10,26},{12,28},{14,30},{16,0},... | collective-permute-start | bytes 196616 | tf_op jit(solution)/shard_map/ppermute | solution.py:543
  38.9 5.2 %collective-permute-start.11 = (f32[1,128,128]{2,1,0:T(8,128)S(1)}, f32[1,128,128]{2,1,0:T(8,128)S(1)}, u32[]{:S(2)}, u32[]{:S(2)}) collective-permute-start(f32[1,128,128]{2,1,0:T(8,128)S(1)} %get-tuple-element.75), channel_id=1, source_target_pairs={{0,16},{2,18},{4,20},{6,22},{8,24},{10,26},{12,28},{14,30},{16,0},... | collective-permute-start | bytes 196616 | tf_op jit(solution)/shard_map/ppermute | solution.py:543
  39.0 11.7 %collective-permute-start.17 = (f32[1,256,128]{2,1,0:T(8,128)S(1)}, f32[1,256,128]{2,1,0:T(8,128)S(1)}, u32[]{:S(2)}, u32[]{:S(2)}) collective-permute-start(f32[1,256,128]{2,1,0:T(8,128)S(1)} %get-tuple-element.89), channel_id=1, source_target_pairs={{0,4},{2,6},{4,0},{6,2},{8,12},{10,14},{12,8},{14,10},{16,20},{18,... | collective-permute-start | bytes 393224 | tf_op jit(solution)/shard_map/ppermute | solution.py:543
  40.5 10.3 %collective-permute-start.16 = (f32[1,256,128]{2,1,0:T(8,128)S(1)}, f32[1,256,128]{2,1,0:T(8,128)S(1)}, u32[]{:S(2)}, u32[]{:S(2)}) collective-permute-start(f32[1,256,128]{2,1,0:T(8,128)S(1)} %get-tuple-element.87), channel_id=1, source_target_pairs={{0,4},{2,6},{4,0},{6,2},{8,12},{10,14},{12,8},{14,10},{16,20},{18,... | collective-permute-start | bytes 393224 | tf_op jit(solution)/shard_map/ppermute | solution.py:543
  41.1 10.4 %collective-permute-start.19 = (f32[1,256,128]{2,1,0:T(8,128)S(1)}, f32[1,256,128]{2,1,0:T(8,128)S(1)}, u32[]{:S(2)}, u32[]{:S(2)}) collective-permute-start(f32[1,256,128]{2,1,0:T(8,128)S(1)} %get-tuple-element.93), channel_id=1, source_target_pairs={{0,4},{2,6},{4,0},{6,2},{8,12},{10,14},{12,8},{14,10},{16,20},{18,... | collective-permute-start | bytes 393224 | tf_op jit(solution)/shard_map/ppermute | solution.py:543
  44.2 7.5 %collective-permute-start.18 = (f32[1,256,128]{2,1,0:T(8,128)S(1)}, f32[1,256,128]{2,1,0:T(8,128)S(1)}, u32[]{:S(2)}, u32[]{:S(2)}) collective-permute-start(f32[1,256,128]{2,1,0:T(8,128)S(1)} %get-tuple-element.91), channel_id=1, source_target_pairs={{0,4},{2,6},{4,0},{6,2},{8,12},{10,14},{12,8},{14,10},{16,20},{18,... | collective-permute-start | bytes 393224 | tf_op jit(solution)/shard_map/ppermute | solution.py:543
  50.8 1.6 %collective-permute-start.21 = (f32[2,1,256,128]{3,2,1,0:T(8,128)S(1)}, f32[2,1,256,128]{3,2,1,0:T(8,128)S(1)}, u32[]{:S(2)}, u32[]{:S(2)}) collective-permute-start(f32[2,1,256,128]{3,2,1,0:T(8,128)S(1)} %get-tuple-element.96), channel_id=1, source_target_pairs={{0,2},{2,0},{4,6},{6,4},{8,10},{10,8},{12,14},{14,12},{16,18},{18,... | collective-permute-start | bytes 786440 | tf_op jit(solution)/shard_map/ppermute | solution.py:543
  51.0 1.8 %collective-permute-start.20 = (f32[2,1,256,128]{3,2,1,0:T(8,128)S(1)}, f32[2,1,256,128]{3,2,1,0:T(8,128)S(1)}, u32[]{:S(2)}, u32[]{:S(2)}) collective-permute-start(f32[2,1,256,128]{3,2,1,0:T(8,128)S(1)} %get-tuple-element.95), channel_id=1, source_target_pairs={{0,2},{2,0},{4,6},{6,4},{8,10},{10,8},{12,14},{14,12},{16,18},{18,... | collective-permute-start | bytes 786440 | tf_op jit(solution)/shard_map/ppermute | solution.py:543
  51.8 1.8 %collective-permute-start.22 = (f32[2,1,256,128]{3,2,1,0:T(8,128)S(1)}, f32[2,1,256,128]{3,2,1,0:T(8,128)S(1)}, u32[]{:S(2)}, u32[]{:S(2)}) collective-permute-start(f32[2,1,256,128]{3,2,1,0:T(8,128)S(1)} %get-tuple-element.97), channel_id=1, source_target_pairs={{0,2},{2,0},{4,6},{6,4},{8,10},{10,8},{12,14},{14,12},{16,18},{18,... | collective-permute-start | bytes 786440 | tf_op jit(solution)/shard_map/ppermute | solution.py:543
  54.8 10.2 %all-to-all-start = ((f32[32,2,32]{2,1,0:T(2,128)}), f32[32,2,32]{2,1,0:T(2,128)S(1)}, u32[]{:S(2)}, u32[]{:S(2)}) async-start(f32[32,2,32]{2,1,0:T(2,128)} %broadcast_in_dim.37), calls=%async_computation | async-start | bytes 65536 | tf_op jit(solution)/shard_map/all_to_all | solution.py:619
  (5 other events, 53.8 us)
